TPU v7x, 256 devices: a whole 4x4x8 slice. The times are simulated.
256 devices in a mesh: row: 32 (over z_hi, x, core), col: 8 (over y, z_lo).
Axes of the slice: x: 4, y: 4, z: 8 (z_hi: 4, z_lo: 2; z = z_hi * 2 + z_lo), core: 2. Of those that a mesh axis runs over, the one named last changes fastest.
Arguments:
- ocean_field: bfloat16 [32, 2048, 2048], P(None, 'row', 'col'), may hold values from -6 to 6
- cotangent: bfloat16 [2048, 2048], P('row', 'col'), may hold values from -6 to 6
- conv_weight: bfloat16 [3, 3, 32, 32], replicated, may hold values from -0.375 to 0.375
- conv_bias: float32 [32], replicated, may hold values from -3 to 3
- projection: float32 [32], replicated, may hold values from -4 to 4
- mode_weight: bfloat16 [128, 2, 32, 32, 256], P('row', None, None, None, 'col'), may hold values from -4.5 to 4.5
Outputs:
- grad_input: float32 [32, 2048, 2048], P(None, 'row', 'col')
- grad_spec: float32 [128, 2, 32, 32, 256], P('row', None, None, None, 'col')
- grad_conv: float32 [3, 3, 32, 32], replicated
- grad_bias: float32 [32], replicated
- grad_proj: float32 [32], replicated
All inputs are finite; a program needn't handle non-finite values.
Results may differ from a plain program's by a relative error of at most 0.0062.
Values may be sent and summed in bfloat16 or wider, within the bound.
A program may use at most 128 MiB of HBM per device.

v0:
```python
import math

import jax
import jax.numpy as jnp
from jax import lax
from jax.sharding import PartitionSpec as P

TWO_PI = 2.0 * math.pi
HIGH = lax.Precision.HIGHEST


def with_halo(array, sides, width):
    for axis, dim in sides:
        devices, length = (lax.axis_size(axis), array.shape[dim])
        up = [(i, (i + 1) % devices) for i in range(devices - 1)]
        down = [(j, i) for i, j in up]
        last = lax.slice_in_dim(array, length - width, length, axis=dim)
        first = lax.slice_in_dim(array, 0, width, axis=dim)
        before = lax.ppermute(last, axis, up)
        after = lax.ppermute(first, axis, down)
        array = jnp.concatenate([before, array, after], axis=dim)
    return array


def angle_pair(products, period):
    angles = (products % period).astype(jnp.float32) * (TWO_PI / period)
    return (jnp.cos(angles).astype(jnp.bfloat16), jnp.sin(angles).astype(jnp.bfloat16))


def column_table(col_ids, modes, period):
    freqs = jnp.arange(modes, dtype=jnp.int32)
    cosine, sine = angle_pair(freqs[:, None] * col_ids[None, :], period)
    return jnp.stack([cosine, -sine], axis=1)


def row_tables(row_ids, kx_ids, modes, period):
    freqs = jnp.where(kx_ids < modes, kx_ids, kx_ids - 2 * modes) % period
    return angle_pair(row_ids[:, None] * freqs[None, :], period)


def column_section(field, col_ids, modes, period):
    table = column_table(col_ids, modes, period)
    return jnp.einsum("cxy,kpy->kpcx", field, table, preferred_element_type=jnp.float32)


def row_section(partial_value, row_ids, kx_ids, modes, period):
    cosine, sine = row_tables(row_ids, kx_ids, modes, period)
    with_cos = jnp.einsum(
        "kpcx,xj->kpcj", partial_value, cosine.astype(jnp.float32), precision=HIGH
    )
    with_sin = jnp.einsum("kpcx,xj->kpcj", partial_value, sine.astype(jnp.float32), precision=HIGH)
    return jnp.stack([with_cos[:, 0] + with_sin[:, 1], with_cos[:, 1] - with_sin[:, 0]], axis=1)


def row_inverse(spectral, row_ids, kx_ids, modes, period):
    cosine, sine = row_tables(row_ids, kx_ids, modes, period)
    with_cos = jnp.einsum("kpcj,xj->kpcx", spectral, cosine, preferred_element_type=jnp.float32)
    with_sin = jnp.einsum("kpcj,xj->kpcx", spectral, sine, preferred_element_type=jnp.float32)
    return jnp.stack([with_cos[:, 0] - with_sin[:, 1], with_cos[:, 1] + with_sin[:, 0]], axis=1)


def column_inverse(summed, weights_ky, col_ids, modes, period, scale):
    table = column_table(col_ids, modes, period).astype(jnp.float32)
    weighted = summed * weights_ky[:, None, None, None]
    return scale * jnp.einsum("kpcx,kpy->cxy", weighted, table, precision=HIGH)


def mix_modes(spectrum, weight):
    wf = weight.astype(jnp.float32)
    real_part = jnp.einsum("kij,kioj->koj", spectrum[:, 0], wf[:, 0], precision=HIGH) - jnp.einsum(
        "kij,kioj->koj", spectrum[:, 1], wf[:, 1], precision=HIGH
    )
    imag_part = jnp.einsum("kij,kioj->koj", spectrum[:, 1], wf[:, 0], precision=HIGH) + jnp.einsum(
        "kij,kioj->koj", spectrum[:, 0], wf[:, 1], precision=HIGH
    )
    return jnp.stack([real_part, imag_part], axis=1)


def mix_back(spectrum, weight, grad_mixed):
    wf = weight.astype(jnp.float32)
    spec_re, spec_im = (spectrum[:, 0], spectrum[:, 1])
    grad_re, grad_im = (grad_mixed[:, 0], grad_mixed[:, 1])
    weight_re = (
        grad_re[:, None, :, :] * spec_re[:, :, None, :]
        + grad_im[:, None, :, :] * spec_im[:, :, None, :]
    )
    weight_im = (
        grad_im[:, None, :, :] * spec_re[:, :, None, :]
        - grad_re[:, None, :, :] * spec_im[:, :, None, :]
    )
    back_re = jnp.einsum("kioj,koj->kij", wf[:, 0], grad_re, precision=HIGH) + jnp.einsum(
        "kioj,koj->kij", wf[:, 1], grad_im, precision=HIGH
    )
    back_im = jnp.einsum("kioj,koj->kij", wf[:, 0], grad_im, precision=HIGH) - jnp.einsum(
        "kioj,koj->kij", wf[:, 1], grad_re, precision=HIGH
    )
    return (
        jnp.stack([weight_re, weight_im], axis=1),
        jnp.stack([back_re, back_im], axis=1).astype(jnp.bfloat16),
    )


def gelu_parts(pre):
    cdf = 0.5 * (1.0 + jax.scipy.special.erf(pre / math.sqrt(2.0)))
    pdf = jnp.exp(-0.5 * pre * pre) / math.sqrt(TWO_PI)
    return (pre * cdf, cdf + pre * pdf)


def conv_cells(padded, kernel, n_rows, n_cols):
    result = jnp.zeros((kernel.shape[3], n_rows, n_cols), jnp.float32)
    for tap_row in range(3):
        for tap_col in range(3):
            shifted = padded[:, tap_row : tap_row + n_rows, tap_col : tap_col + n_cols]
            result = result + jnp.einsum(
                "io,ixy->oxy", kernel[tap_row, tap_col], shifted, preferred_element_type=jnp.float32
            )
    return result


def conv_transpose(padded, kernel, n_rows, n_cols):
    result = jnp.zeros((kernel.shape[2], n_rows, n_cols), jnp.float32)
    for tap_row in range(3):
        for tap_col in range(3):
            shifted = padded[
                :, 2 - tap_row : 2 - tap_row + n_rows, 2 - tap_col : 2 - tap_col + n_cols
            ]
            result = result + jnp.einsum(
                "io,oxy->ixy", kernel[tap_row, tap_col], shifted, preferred_element_type=jnp.float32
            )
    return result


def kernel_grad(padded, grad_round, n_rows, n_cols):
    taps = []
    for tap_row in range(3):
        for tap_col in range(3):
            shifted = padded[:, tap_row : tap_row + n_rows, tap_col : tap_col + n_cols]
            taps.append(
                jnp.einsum("ixy,oxy->io", shifted, grad_round, preferred_element_type=jnp.float32)
            )
    return jnp.stack(taps).reshape(3, 3, padded.shape[0], grad_round.shape[0])


def per_device(ocean_field, cotangent, conv_weight, conv_bias, projection, mode_weight):
    chans, rows_dev, cols_dev = ocean_field.shape
    n_row = lax.axis_size("row")
    n_col = lax.axis_size("col")
    ky_dev = mode_weight.shape[0]
    kx_dev = mode_weight.shape[4]
    modes = ky_dev * n_row
    kx_all = kx_dev * n_col
    nx_all = rows_dev * n_row
    ny_all = cols_dev * n_col
    strip_rows = rows_dev // n_col
    row_at = lax.axis_index("row")
    col_at = lax.axis_index("col")
    scale = 1.0 / math.sqrt(nx_all * ny_all)
    my_cols = col_at * cols_dev + jnp.arange(cols_dev, dtype=jnp.int32)
    my_ky = row_at * ky_dev + jnp.arange(ky_dev, dtype=jnp.int32)
    kx_every = jnp.arange(kx_all, dtype=jnp.int32)
    set_rows = (
        jnp.arange(n_row, dtype=jnp.int32)[:, None] * rows_dev
        + col_at * strip_rows
        + jnp.arange(strip_rows, dtype=jnp.int32)[None, :]
    ).reshape(-1)
    ky_weight = jnp.where(jnp.arange(modes) == 0, 1.0, 2.0).astype(jnp.float32)
    mine_weight = jnp.where(my_ky == 0, 1.0, 2.0).astype(jnp.float32)

    def column_sums(field):
        partial_value = column_section(field, my_cols, modes, ny_all)
        return lax.psum_scatter(partial_value, "col", scatter_dimension=3, tiled=True)

    def forward_modes(field):
        whole_y = column_sums(field)
        by_ky = row_section(
            lax.all_to_all(whole_y, "row", split_axis=0, concat_axis=3, tiled=True),
            set_rows,
            kx_every,
            modes,
            nx_all,
        )
        return lax.psum_scatter(by_ky, "col", scatter_dimension=3, tiled=True)

    def to_grid(spectral, weights_ky):
        pieces = lax.all_gather(spectral, "col", axis=3, tiled=True)
        kx_ids = jnp.arange(pieces.shape[3], dtype=jnp.int32)
        summed = row_inverse(pieces, set_rows, kx_ids, modes, nx_all)
        returned = lax.all_to_all(summed, "row", split_axis=3, concat_axis=0, tiled=True)
        return column_inverse(
            lax.all_gather(returned, "col", axis=3, tiled=True),
            weights_ky,
            my_cols,
            modes,
            ny_all,
            scale,
        )

    padded_in = with_halo(ocean_field, (("row", 1), ("col", 2)), 1)
    spectrum = forward_modes(ocean_field) * scale
    mixed = mix_modes(spectrum, mode_weight).astype(jnp.bfloat16)
    spectral_cells = to_grid(mixed, ky_weight)
    pre_act = (
        conv_cells(padded_in, conv_weight, rows_dev, cols_dev)
        + spectral_cells
        + conv_bias[:, None, None]
    )
    activ, slope = gelu_parts(pre_act)
    cot_rows = cotangent.astype(jnp.float32)
    grad_pre = projection[:, None, None] * cot_rows[None] * slope
    grad_round = grad_pre.astype(jnp.bfloat16)
    kernel_part = kernel_grad(padded_in, grad_round, rows_dev, cols_dev)
    bias_part = jnp.sum(grad_pre, axis=(1, 2))
    proj_part = jnp.sum(activ * cot_rows[None], axis=(1, 2))
    kernel_sum, bias_sum, proj_sum = lax.psum((kernel_part, bias_part, proj_part), ("row", "col"))
    grad_modes = forward_modes(grad_round) * (scale * mine_weight)[:, None, None, None]
    grad_spec, grad_spectrum = mix_back(spectrum, mode_weight, grad_modes)
    padded_grad = with_halo(grad_round, (("row", 1), ("col", 2)), 1)
    back_cells = conv_transpose(padded_grad, conv_weight, rows_dev, cols_dev)
    spectral_back = to_grid(grad_spectrum, jnp.ones((modes,), jnp.float32))
    grad_input = back_cells + spectral_back
    return (grad_input, grad_spec, kernel_sum * scale, bias_sum * scale, proj_sum * scale)


def solution(mesh):
    placed = (
        P(None, "row", "col"),
        P("row", "col"),
        P(),
        P(),
        P(),
        P("row", None, None, None, "col"),
    )
    return jax.shard_map(
        per_device,
        mesh=mesh,
        in_specs=placed,
        out_specs=(P(None, "row", "col"), P("row", None, None, None, "col"), P(), P(), P()),
        check_vma=False,
    )
```

profile of v0, /device:TPU:1, one launch (start us, length us, event | category | flops | bytes accessed | tf_op | source)
XLA Modules:
  0.0 567.8 jit_solution(2146350703683208612)
XLA Ops:
  8.2 3.0 fusion.69
  11.3 58.9 %reduce-scatter.9.cloned.1.call-done = f32[128,2,32,8]{0,3,2,1:T(8,128)} async-done(((f32[128,2,32,64]{0,3,2,1:T(8,128)}), f32[128,2,32,8]{0,3,2,1:T(8,128)}) %reduce-scatter.9.cloned.1.call-update) | async-done | bytes 262160 | tf_op jit(solution)/shard_map/reduce_scatter | solution.py:171
  72.8 9.5 %all-to-all-start = ((f32[32,1,2048]{2,1,0:T(1,128)}), f32[32,1,2048]{2,1,0:T(1,128)S(1)}, u32[]{:S(2)}, u32[]{:S(2)}) async-start(f32[32,1,2048]{2,1,0:T(1,128)} %reshape.249), calls=%async_computation.1 | async-start | bytes 524288 | tf_op jit(solution)/shard_map/all_to_all | solution.py:176
  82.5 12.7 %all-to-all-done = f32[32,1,2048]{2,1,0:T(1,128)S(1)} async-done(((f32[32,1,2048]{2,1,0:T(1,128)}), f32[32,1,2048]{2,1,0:T(1,128)S(1)}, u32[]{:S(2)}, u32[]{:S(2)}) %all-to-all-start) | async-done | bytes 262176 | tf_op jit(solution)/shard_map/all_to_all | solution.py:176
  103.6 1.9 reshape.245
  105.6 28.5 %reduce-scatter.13.cloned.1.call-done = f32[32,256]{1,0:T(8,128)} async-done(((f32[256,256]{1,0:T(8,128)}), f32[32,256]{1,0:T(8,128)}) %reduce-scatter.13.cloned.1.call-update) | async-done | bytes 32784
  137.2 23.5 %all_gather.12 = bf16[4,2,32,256]{2,0,1,3:T(4,128)(2,1)S(1)} all-gather(bf16[4,2,32,32]{2,0,1,3:T(4,128)(2,1)S(1)} %pad_maximum_fusion.14), channel_id=1, replica_groups=mesh['row'=32,'col'=8] {'col'}, dimensions={3}, use_global_device_ids=true | all-gather | bytes 147456 | tf_op jit(solution)/shard_map/all_gather | solution.py:185
  165.4 33.7 %all_to_all.72 = f32[32,1,2048]{2,1,0:T(1,128)S(1)} all-to-all(f32[32,1,2048]{2,1,0:T(1,128)S(1)} %reshape.251), channel_id=1, replica_groups=mesh['row'=32,'col'=8] {'row'}, dimensions={0} | all-to-all | bytes 524288 | tf_op jit(solution)/shard_map/all_to_all | solution.py:188
  202.9 1.9 collective-permute-start.1
  204.9 3.6 collective-permute-start
  208.5 2.1 fusion.120
  219.0 3.0 fusion.55
  222.0 3.0 fusion.57
  227.7 1.9 fusion.76
  229.5 1.9 fusion.131
  231.4 1.9 fusion.123
  233.3 2.0 fusion.126
  235.3 2.0 fusion.116
  237.4 11.8 %all-gather.3.cloned.1.call-done = f32[128,2,32,64]{0,3,2,1:T(8,128)} async-done(((f32[128,2,32,8]{0,3,2,1:T(8,128)}), f32[128,2,32,64]{0,3,2,1:T(8,128)}) %all-gather.3.cloned.1.call-update) | async-done | bytes 2097168 | tf_op jit(solution)/shard_map/all_gather | solution.py:190
  249.2 1.9 broadcast_multiply_fusion
  251.1 2.5 fusion.16
  253.7 6.1 %multiply_reduce_fusion = (f32[32]{0:T(128)}, f32[32]{0:T(128)}, f32[32,64,256]{2,0,1:T(8,128)S(1)}, f32[32,64,256]{2,0,1:T(8,128)S(1)}) fusion(f32[64,256]{1,0:T(8,128)S(1)} %convert_element_type.77, f32[32]{0:T(128)S(1)} %copy-done.26, f32[32]{0:T(128)S(1)} %copy-done.29, f32[32,64,256,1]{2,0,3,1:T(8,128)S(1)} %fusion.16, ...), kind=kOutput, calls=%fused_computation.37 | convolution fusion | flops 48758720 | bytes 24765696 | tf_op jit(solution)/shard_map/io,ixy->oxy/dot_general | solution.py:114
  260.5 2.6 fusion.63
  263.8 3.8 collective-permute-start.5
  267.6 3.4 collective-permute-start.4
  271.0 2.2 fusion.28
  276.7 42.5 %reduce-scatter.11.cloned.1.call-done = f32[128,2,32,8]{0,3,2,1:T(8,128)} async-done(((f32[128,2,32,64]{0,3,2,1:T(8,128)}), f32[128,2,32,8]{0,3,2,1:T(8,128)}) %reduce-scatter.11.cloned.1.call-update) | async-done | bytes 262160 | tf_op jit(solution)/shard_map/reduce_scatter | solution.py:171
  319.2 2.3 copy.252
  321.5 2.4 reshape.253
  323.9 9.6 %all-to-all-start.2 = ((f32[32,1,2048]{2,1,0:T(1,128)}), f32[32,1,2048]{2,1,0:T(1,128)}, u32[]{:S(2)}, u32[]{:S(2)}) async-start(f32[32,1,2048]{2,1,0:T(1,128)} %reshape.253), calls=%async_computation.4 | async-start | bytes 524288 | tf_op jit(solution)/shard_map/all_to_all | solution.py:176
  337.5 9.1 %all-to-all-done.2 = f32[32,1,2048]{2,1,0:T(1,128)} async-done(((f32[32,1,2048]{2,1,0:T(1,128)}), f32[32,1,2048]{2,1,0:T(1,128)}, u32[]{:S(2)}, u32[]{:S(2)}) %all-to-all-start.2) | async-done | bytes 262176 | tf_op jit(solution)/shard_map/all_to_all | solution.py:176
  346.6 2.9 reduce.18
  355.2 2.1 copy.366
  357.4 3.1 reshape.247
  362.9 74.9 %all-reduce = (f32[3,3,32,32]{3,2,1,0:T(8,128)}, f32[32]{0:T(128)S(1)}, f32[32]{0:T(128)S(1)}) all-reduce(f32[3,3,32,32]{3,2,1,0:T(8,128)} %bitcast.123, f32[32]{0:T(128)S(1)} %copy-done.28, f32[32]{0:T(128)S(1)} %copy-done.27), channel_id=1, replica_groups=mesh['row'=32,'col'=8] {'row','col'}, use_global_device_ids=true, to_apply=%region_4.5 | all-reduce | flops 9280 | bytes 74240 | tf_op jit(solution)/shard_map/psum | solution.py:214
  439.5 3.4 fusion.6
  443.5 24.6 %all_gather.14 = bf16[4,2,32,256]{2,0,1,3:T(4,128)(2,1)S(1)} all-gather(bf16[4,2,32,32]{2,0,1,3:T(4,128)(2,1)S(1)} %pad_maximum_fusion.15), channel_id=1, replica_groups=mesh['row'=32,'col'=8] {'col'}, dimensions={3}, use_global_device_ids=true | all-gather | bytes 147456 | tf_op jit(solution)/shard_map/all_gather | solution.py:185
  473.4 11.0 %all-to-all-start.3 = ((f32[32,1,2048]{2,1,0:T(1,128)}), f32[32,1,2048]{2,1,0:T(1,128)S(1)}, u32[]{:S(2)}, u32[]{:S(2)}) async-start(f32[32,1,2048]{2,1,0:T(1,128)} %reshape.255), calls=%async_computation.5 | async-start | bytes 524288 | tf_op jit(solution)/shard_map/all_to_all | solution.py:188
  486.9 10.3 %all-to-all-done.3 = f32[32,1,2048]{2,1,0:T(1,128)S(1)} async-done(((f32[32,1,2048]{2,1,0:T(1,128)}), f32[32,1,2048]{2,1,0:T(1,128)S(1)}, u32[]{:S(2)}, u32[]{:S(2)}) %all-to-all-start.3) | async-done | bytes 262176 | tf_op jit(solution)/shard_map/all_to_all | solution.py:188
  506.0 4.0 collective-permute-start.7
  510.0 2.5 fusion.33
  516.9 2.3 maximum_maximum_fusion
  522.7 1.9 fusion.45
  528.9 2.9 pad_maximum_fusion
  531.8 15.7 %all-gather.5.cloned.1.call-done = f32[128,2,32,64]{0,3,1,2:T(8,128)} async-done(((f32[128,2,32,8]{0,3,1,2:T(8,128)}), f32[128,2,32,64]{0,3,1,2:T(8,128)}) %all-gather.5.cloned.1.call-update) | async-done | bytes 2097168 | tf_op jit(solution)/shard_map/all_gather | solution.py:190
  547.5 4.2 fusion.18
  551.7 6.3 %fusion.13 = f32[32,64,256]{2,0,1:T(8,128)S(1)} fusion(f32[32,64,256,1]{2,0,3,1:T(8,128)S(1)} %fusion.18, f32[64,256,32]{1,2,0:T(8,128)S(1)} %copy-done.12, f32[64,256,32]{1,2,0:T(8,128)} %fusion.45, f32[64,256,32]{1,2,0:T(8,128)} %fusion.47, f32[64,256,32]{1,2,0:T(8,128)S(1)} %copy-done.11, f32[64,256,32]{1,2,0:T(8,128)} %fusion.49, ...), kind=kOutput, calls=%fused_computation.24 | convolution fusion | flops 38797312 | bytes 22028288 | tf_op jit(solution)/shard_map/io,oxy->ixy/dot_general | solution.py:127
  558.0 2.5 copy.265
  (192 shorter events, 82.4 us)
Async XLA Ops:
  7.2 63.0 %reduce-scatter.9.cloned.1.call-start = ((), (), s32[]{:S(2)}) async-start(), calls=%async_computation.8 | async-start | bytes 2359296 | tf_op jit(solution)/shard_map/reduce_scatter | solution.py:171
  72.8 22.5 %all-to-all-start = ((f32[32,1,2048]{2,1,0:T(1,128)}), f32[32,1,2048]{2,1,0:T(1,128)S(1)}, u32[]{:S(2)}, u32[]{:S(2)}) async-start(f32[32,1,2048]{2,1,0:T(1,128)} %reshape.249), calls=%async_computation.1 | async-start | bytes 524288 | tf_op jit(solution)/shard_map/all_to_all | solution.py:176
  82.3 51.8 %reduce-scatter.13.cloned.1.call-start = ((), (), s32[]{:S(2)}) async-start(), calls=%async_computation.12 | async-start | bytes 294912
  101.8 33.9 %copy-start.13 = (bf16[4,2,32,32,32]{4,3,2,1,0:T(8,128)(2,1)S(1)}, bf16[4,2,32,32,32]{4,3,2,1,0:T(8,128)(2,1)}, u32[]{:S(2)}) copy-start(bf16[4,2,32,32,32]{4,3,2,1,0:T(8,128)(2,1)} %param.11) | copy-start | bytes 1572868
  105.6 143.6 %all-gather.3.cloned.1.call-start = ((), (), s32[]{:S(2)}) async-start(), calls=%async_computation.9 | async-start | bytes 2359296 | tf_op jit(solution)/shard_map/all_gather | solution.py:190
  201.5 1.4 copy-start
  201.5 7.0 %copy-start.19 = (bf16[3,3,32,32]{3,2,1,0:T(8,128)(2,1)S(1)}, bf16[3,3,32,32]{3,2,1,0:T(8,128)(2,1)}, u32[]{:S(2)}) copy-start(bf16[3,3,32,32]{3,2,1,0:T(8,128)(2,1)} %param.8) | copy-start | bytes 55300
  202.8 7.8 %copy-start.25 = (bf16[64,256]{1,0:T(8,128)(2,1)S(1)}, bf16[64,256]{1,0:T(8,128)(2,1)}, u32[]{:S(2)}) copy-start(bf16[64,256]{1,0:T(8,128)(2,1)} %param.7) | copy-start | bytes 98308
  202.8 116.4 %reduce-scatter.11.cloned.1.call-start = ((), (), s32[]{:S(2)}) async-start(), calls=%async_computation.10 | async-start | bytes 2359296 | tf_op jit(solution)/shard_map/reduce_scatter | solution.py:171
  202.9 8.4 %collective-permute-start.1 = (bf16[32,1,256]{2,0,1:T(8,128)(2,1)S(1)}, bf16[32,1,256]{2,0,1:T(8,128)(2,1)S(1)}, u32[]{:S(2)}, u32[]{:S(2)}) collective-permute-start(bf16[32,1,256]{2,0,1:T(8,128)(2,1)S(1)} %copy.414), channel_id=1, source_target_pairs={{8,0},{16,8},{24,16},{32,24},{40,32},{48,40},{56,48},{64,56},{72,6... | collective-permute-start | bytes 49160 | tf_op jit(solution)/shard_map/ppermute | solution.py:20
  204.9 5.7 %collective-permute-start = (bf16[32,1,256]{2,0,1:T(8,128)(2,1)S(1)}, bf16[32,1,256]{2,0,1:T(8,128)(2,1)S(1)}, u32[]{:S(2)}, u32[]{:S(2)}) collective-permute-start(bf16[32,1,256]{2,0,1:T(8,128)(2,1)S(1)} %copy.415), channel_id=1, source_target_pairs={{0,8},{8,16},{16,24},{24,32},{32,40},{40,48},{48,56},{56,64},{64,7... | collective-permute-start | bytes 49160 | tf_op jit(solution)/shard_map/ppermute | solution.py:19
  211.3 1.3 copy-start.17
  211.3 1.1 copy-start.1
  216.0 10.7 %collective-permute-start.2 = (bf16[32,66,1]{1,0,2:T(8,128)(2,1)S(1)}, bf16[32,66,1]{1,0,2:T(8,128)(2,1)S(1)}, u32[]{:S(2)}, u32[]{:S(2)}) collective-permute-start(bf16[32,66,1]{1,0,2:T(8,128)(2,1)S(1)} %copy.210), channel_id=1, source_target_pairs={{0,1},{1,2},{2,3},{3,4},{4,5},{5,6},{6,7},{8,9},{9,10},{10,11},{11... | collective-permute-start | bytes 12680 | tf_op jit(solution)/shard_map/ppermute | solution.py:19
  217.3 7.7 %collective-permute-start.3 = (bf16[32,66,1]{1,0,2:T(8,128)(2,1)S(1)}, bf16[32,66,1]{1,0,2:T(8,128)(2,1)S(1)}, u32[]{:S(2)}, u32[]{:S(2)}) collective-permute-start(bf16[32,66,1]{1,0,2:T(8,128)(2,1)S(1)} %copy.215), channel_id=1, source_target_pairs={{1,0},{2,1},{3,2},{4,3},{5,4},{6,5},{7,6},{9,8},{10,9},{11,10},{12... | collective-permute-start | bytes 12680 | tf_op jit(solution)/shard_map/ppermute | solution.py:20
  227.7 3.7 copy-start.3
  231.4 1.9 copy-start.6
  249.2 4.5 copy-start.15
  249.2 4.5 copy-start.16
  251.1 2.6 copy-start.7
  251.1 2.6 copy-start.14
  251.1 2.6 copy-start.26
  251.1 2.6 copy-start.29
  263.1 10.1 %copy-start.18 = (bf16[32,65,256]{2,0,1:T(8,128)(2,1)S(1)}, bf16[32,65,256]{2,0,1:T(8,128)(2,1)}, u32[]{:S(2)}) copy-start(bf16[32,65,256]{2,0,1:T(8,128)(2,1)} %copy-done.17) | copy-start | bytes 3194884
  263.8 238.2 %collective-permute-start.5 = (bf16[32,1,256]{2,0,1:T(8,128)(2,1)}, bf16[32,1,256]{2,0,1:T(8,128)(2,1)S(1)}, u32[]{:S(2)}, u32[]{:S(2)}) collective-permute-start(bf16[32,1,256]{2,0,1:T(8,128)(2,1)} %get-tuple-element.54), channel_id=1, source_target_pairs={{8,0},{16,8},{24,16},{32,24},{40,32},{48,40},{56,48},{64,56},{72,6... | collective-permute-start | bytes 49160 | tf_op jit(solution)/shard_map/ppermute | solution.py:20
  267.6 6.6 %copy-start.8 = (bf16[32,66,1]{2,0,1:T(8,128)(2,1)S(1)}, bf16[32,66,1]{2,0,1:T(8,128)(2,1)}, u32[]{:S(2)}) copy-start(bf16[32,66,1]{2,0,1:T(8,128)(2,1)} %copy.216) | copy-start | bytes 12676
  267.6 234.4 %collective-permute-start.4 = (bf16[32,1,256]{2,0,1:T(8,128)(2,1)}, bf16[32,1,256]{2,0,1:T(8,128)(2,1)}, u32[]{:S(2)}, u32[]{:S(2)}) collective-permute-start(bf16[32,1,256]{2,0,1:T(8,128)(2,1)} %get-tuple-element.55), channel_id=1, source_target_pairs={{0,8},{8,16},{16,24},{24,32},{32,40},{40,48},{48,56},{56,64},{64,7... | collective-permute-start | bytes 49160 | tf_op jit(solution)/shard_map/ppermute | solution.py:19
  274.2 1.3 copy-start.4
  323.9 22.7 %all-to-all-start.2 = ((f32[32,1,2048]{2,1,0:T(1,128)}), f32[32,1,2048]{2,1,0:T(1,128)}, u32[]{:S(2)}, u32[]{:S(2)}) async-start(f32[32,1,2048]{2,1,0:T(1,128)} %reshape.253), calls=%async_computation.4 | async-start | bytes 524288 | tf_op jit(solution)/shard_map/all_to_all | solution.py:176
  333.5 104.2 %reduce-scatter.15.cloned.1.call-start = ((), (), s32[]{:S(2)}) async-start(), calls=%async_computation.13 | async-start | bytes 294912
  333.6 1.5 copy-start.9
  335.0 1.3 copy-start.5
  354.5 6.1 %copy-start.2 = (bf16[32,65,256]{2,0,1:T(8,128)(2,1)S(1)}, bf16[32,65,256]{2,0,1:T(8,128)(2,1)}, u32[]{:S(2)}) copy-start(bf16[32,65,256]{2,0,1:T(8,128)(2,1)} %copy-done.1) | copy-start | bytes 3194884
  360.5 1.1 copy-start.10
  360.5 2.4 copy-start.27
  360.6 2.3 copy-start.28
  470.9 13.6 %copy-start.24 = (f32[3,3,32,32]{3,2,1,0:T(8,128)S(1)}, f32[3,3,32,32]{3,2,1,0:T(8,128)}, u32[]{:S(2)}) copy-start(f32[3,3,32,32]{3,2,1,0:T(8,128)} %get-tuple-element.44) | copy-start | bytes 110596
  473.4 23.8 %all-to-all-start.3 = ((f32[32,1,2048]{2,1,0:T(1,128)}), f32[32,1,2048]{2,1,0:T(1,128)S(1)}, u32[]{:S(2)}, u32[]{:S(2)}) async-start(f32[32,1,2048]{2,1,0:T(1,128)} %reshape.255), calls=%async_computation.5 | async-start | bytes 524288 | tf_op jit(solution)/shard_map/all_to_all | solution.py:188
  484.4 63.1 %all-gather.5.cloned.1.call-start = ((), (), s32[]{:S(2)}) async-start(), calls=%async_computation.11 | async-start | bytes 2359296 | tf_op jit(solution)/shard_map/all_gather | solution.py:190
  502.0 10.5 %copy-start.23 = (bf16[32,1,256]{2,0,1:T(8,128)(2,1)}, bf16[32,1,256]{2,0,1:T(8,128)(2,1)S(1)}, u32[]{:S(2)}) copy-start(bf16[32,1,256]{2,0,1:T(8,128)(2,1)S(1)} %collective-permute-done.5) | copy-start | bytes 49156
  504.5 10.7 %collective-permute-start.6 = (bf16[32,66,1]{1,0,2:T(8,128)(2,1)S(1)}, bf16[32,66,1]{1,0,2:T(8,128)(2,1)S(1)}, u32[]{:S(2)}, u32[]{:S(2)}) collective-permute-start(bf16[32,66,1]{1,0,2:T(8,128)(2,1)S(1)} %copy.238), channel_id=1, source_target_pairs={{1,0},{2,1},{3,2},{4,3},{5,4},{6,5},{7,6},{9,8},{10,9},{11,10},{12... | collective-permute-start | bytes 12680 | tf_op jit(solution)/shard_map/ppermute | solution.py:20
  506.0 8.2 %collective-permute-start.7 = (bf16[32,66,1]{1,0,2:T(8,128)(2,1)S(1)}, bf16[32,66,1]{1,0,2:T(8,128)(2,1)S(1)}, u32[]{:S(2)}, u32[]{:S(2)}) collective-permute-start(bf16[32,66,1]{1,0,2:T(8,128)(2,1)S(1)} %copy.242), channel_id=1, source_target_pairs={{0,1},{1,2},{2,3},{3,4},{4,5},{5,6},{6,7},{8,9},{9,10},{10,11},{11... | collective-permute-start | bytes 12680 | tf_op jit(solution)/shard_map/ppermute | solution.py:19
  526.4 1.8 copy-start.20
  526.4 1.8 copy-start.21
  526.4 1.8 copy-start.22
  547.5 4.2 copy-start.11
  547.5 4.2 copy-start.12
Sparse Core Ops, SparseCore 0:
  11.4 58.7 reduce-scatter.8
  105.7 28.3 reduce-scatter.12
  202.9 46.2 all-gather.2
  263.3 55.9 reduce-scatter.10
  360.6 28.4 reduce-scatter.14
  501.1 46.3 all-gather.4
where the time goes:
time: 577 us; the launch traced here: 568 us
  waiting for transfers between devices  190 us (33%)
  blocking collectives  157 us (27%)
  matrix products  81.5 us (14%)
  starting transfers between devices  51.6 us (9%)
  local copies, waits for them, and re-layouts  47.8 us (8%)
  other arithmetic  25.1 us (4%)
  between operations  15.5 us (3%)
    reduce_scatter x2, waiting for transfers between devices, column_sums(): lax.psum_scatter(partial_value, 'col', scatter_dimension=3, tiled=True)  101 us
    psum x1, blocking collectives, per_device(): lax.psum((kernel_part, bias_part, proj_part), ('row', 'col'))  74.9 us
    all_gather x2, blocking collectives, to_grid(): pieces = lax.all_gather(spectral, 'col', axis=3, tiled=True)  48.2 us
    all_to_all x1, blocking collectives, to_grid(): lax.all_to_all(summed, 'row', split_axis=3, concat_axis=0, tiled=True)  33.7 us
    unnamed x8, waiting for transfers between devices  28.6 us
    all_gather x2, waiting for transfers between devices, to_grid(): lax.all_gather(returned, 'col', axis=3, tiled=True)  27.5 us
    unnamed x80, local copies, waits for them, and re-layouts  24.7 us
    dot_general x9, matrix products, conv_cells(): jnp.einsum('io,ixy->oxy', kernel[tap_row, tap_col], shifted, preferred_el...  23.8 us
  transfers between devices with their start and end apart: 17, of which 8 were waited for; matrix products, arithmetic and copies ran while one was open for 17% of the time, Pallas kernels for 0%

commit v1 on v0

v1 whole, which is shorter than its diff:
```python
import functools
import math

import jax
import jax.numpy as jnp
import ml_dtypes
import numpy as np
from jax import lax
from jax.experimental import pallas as pl
from jax.experimental.pallas import tpu as pltpu
from jax.sharding import PartitionSpec as P

TWO_PI = 2.0 * math.pi
VMEM_BYTES = 56 * 1024 * 1024


def with_halo(array, sides, width):
    for axis, dim in sides:
        devices, length = (lax.axis_size(axis), array.shape[dim])
        up = [(i, (i + 1) % devices) for i in range(devices - 1)]
        down = [(j, i) for i, j in up]
        last = lax.slice_in_dim(array, length - width, length, axis=dim)
        first = lax.slice_in_dim(array, 0, width, axis=dim)
        before = lax.ppermute(last, axis, up)
        after = lax.ppermute(first, axis, down)
        array = jnp.concatenate([before, array, after], axis=dim)
    return array


def angle_pair(products, period):
    angles = (products % period).astype(np.float32) * np.float32(TWO_PI / period)
    return (np.cos(angles).astype(ml_dtypes.bfloat16), np.sin(angles).astype(ml_dtypes.bfloat16))


def tables(n_row, n_col, ky_dev, rows_dev, cols_dev, kx_all):
    modes, nx, ny = (ky_dev * n_row, rows_dev * n_row, cols_dev * n_col)
    cosine, sine = angle_pair(np.arange(modes)[:, None] * np.arange(ny)[None, :], ny)
    ty = np.stack([cosine.reshape(n_row, ky_dev, ny), -sine.reshape(n_row, ky_dev, ny)], axis=1)
    ty = ty.reshape(2 * modes, n_col, cols_dev).transpose(1, 0, 2)
    ids = np.arange(kx_all)
    freqs = np.where(ids < modes, ids, ids - 2 * modes) % nx
    cosine, sine = angle_pair(freqs[:, None] * np.arange(nx)[None, :], nx)
    return np.ascontiguousarray(ty), np.concatenate([cosine, sine], axis=0)


NT = (((1,), (1,)), ((), ()))
NN = (((1,), (0,)), ((), ()))


def dot(a, b, dims):
    return lax.dot_general(a, b, dims, preferred_element_type=jnp.float32)


def exchange(axis, me, size, source, target, send_sem, recv_sem):
    def copy(step, peer, slot):
        return pltpu.make_async_remote_copy(
            src_ref=source(peer),
            dst_ref=target(slot),
            send_sem=send_sem.at[step],
            recv_sem=recv_sem.at[step],
            device_id={axis: peer},
            device_id_type=pl.DeviceIdType.MESH,
        )

    def start(step):
        copy(step, lax.rem(me + step, size), me).start()

    def wait_send(step):
        copy(step, lax.rem(me + step, size), me).wait_send()

    def wait_recv(step):
        origin = lax.rem(me + size - step, size)
        copy(step, lax.rem(me + step, size), origin).wait_recv()
        return origin

    return start, wait_send, wait_recv


def each(size, body):
    def step(index, carry):
        body(index)
        return carry

    lax.fori_loop(1, size, step, 0)


def part_swap(value, sign):
    rows = value.shape[0]
    is_real = (lax.broadcasted_iota(jnp.int32, value.shape, 0) & 4) == 0
    after = pltpu.roll(value, rows - 4, 0)
    before = pltpu.roll(value, 4, 0)
    return jnp.where(is_real, sign * after, -sign * before)


def chain_kernel(forward, n_row, n_col, *refs):
    if forward:
        (v_ref, w_ref, ty_ref, tx_ref, cells_ref, spec_ref, *scratch) = refs
    else:
        (v_ref, w_ref, ty_ref, tx_ref, spec_ref, cells_ref, gspec_ref, *scratch) = refs
    (buf1, acc, snd3, rcv3, rows_x, snd5, rcv5, modes_ref, mix_ref, snd7, rcv7, snd9, rcv9, snd10, rcv10,
     local_sem, s1, r1, s3, r3, s5, r5, s7, r7, s9, r9, s10, r10) = scratch
    row_at = lax.axis_index("row")
    col_at = lax.axis_index("col")
    pairs = n_row // 2
    scale = 1.0 / math.sqrt((64 * n_row) * (256 * n_col))

    own = pltpu.make_async_copy(v_ref.at[col_at], buf1.at[col_at], local_sem)
    own.start()
    barrier = pltpu.get_barrier_semaphore()
    each(n_col, lambda d: pl.semaphore_signal(
        barrier, inc=1, device_id={"col": lax.rem(col_at + d, n_col)}, device_id_type=pl.DeviceIdType.MESH))
    each(n_row, lambda d: pl.semaphore_signal(
        barrier, inc=1, device_id={"row": lax.rem(row_at + d, n_row)}, device_id_type=pl.DeviceIdType.MESH))
    pl.semaphore_wait(barrier, n_col - 1 + n_row - 1)

    start1, sent1, got1 = exchange("col", col_at, n_col, lambda i: v_ref.at[i], lambda i: buf1.at[i], s1, r1)
    each(n_col, start1)
    own.wait()
    acc[...] = dot(ty_ref[col_at], buf1[col_at], NT)

    def add_block(d):
        origin = got1(d)
        acc[...] += dot(ty_ref[origin], buf1[origin], NT)

    each(n_col, add_block)

    whole = acc[...]
    left = whole[:, :128].reshape(n_row, 8, 128)
    right = whole[:, 128:].reshape(n_row, 8, 128)
    snd3[...] = jnp.concatenate([left, right], axis=1).astype(jnp.bfloat16)
    start3, sent3, got3 = exchange("row", row_at, n_row, lambda i: snd3.at[i], lambda i: rcv3.at[i], s3, r3)
    each(n_row, start3)
    rcv3[row_at] = snd3[row_at]
    each(n_row, got3)

    low = lax.broadcasted_iota(jnp.int32, (16, 128), 1) < 64
    for s in range(pairs):
        first = rcv3[2 * s].astype(jnp.float32)
        second = rcv3[2 * s + 1].astype(jnp.float32)
        even = jnp.where(low, first, pltpu.roll(second, 64, 1))
        odd = jnp.where(low, pltpu.roll(first, 64, 1), second)
        rows_x[0:16, 128 * s : 128 * s + 128] = even.astype(jnp.bfloat16)
        rows_x[16:32, 128 * s : 128 * s + 128] = odd.astype(jnp.bfloat16)
    both = dot(rows_x[...], tx_ref[...], NT)
    coeffs = (both[:, :256] + part_swap(both[:, 256:], 1.0)) * scale
    coeffs = jnp.concatenate([coeffs[0:8], coeffs[16:24], coeffs[8:16], coeffs[24:32]], axis=0)
    snd5[0] = coeffs[:, :128].astype(jnp.bfloat16)
    snd5[1] = coeffs[:, 128:].astype(jnp.bfloat16)
    start5, sent5, got5 = exchange("col", col_at, n_col, lambda i: snd5.at[i // 4], lambda i: rcv5.at[i], s5, r5)
    each(n_col, start5)
    rcv5[col_at] = snd5[col_at // 4]
    each(n_col, got5)
    quarter = lax.rem(col_at, 4) * 32
    back_shift = lax.rem(128 - quarter, 128)
    for i in range(n_col):
        modes_ref[32 * i : 32 * i + 32] = pltpu.roll(rcv5[i].astype(jnp.float32), back_shift, 1)

    mix_ref[...] = jnp.zeros_like(mix_ref)
    if forward:
        spec_ref[...] = modes_ref[...]
        for kl in range(4):

            def add_channel(i, sums):
                real, imag = sums
                s_re = modes_ref[pl.ds(8 * i + kl, 1), :][:, :32]
                s_im = modes_ref[pl.ds(8 * i + 4 + kl, 1), :][:, :32]
                w_re = w_ref[kl, 0, i].astype(jnp.float32)
                w_im = w_ref[kl, 1, i].astype(jnp.float32)
                return (real + (w_re * s_re - w_im * s_im), imag + (w_re * s_im + w_im * s_re))

            zero = jnp.zeros((32, 32), jnp.float32)
            real, imag = lax.fori_loop(0, 32, add_channel, (zero, zero))
            factor = jnp.where(row_at * 4 + kl == 0, 1.0, 2.0).astype(jnp.float32) * scale
            mix_ref[32 * kl : 32 * kl + 32, 0:32] = real.astype(jnp.bfloat16).astype(jnp.float32) * factor
            mix_ref[128 + 32 * kl : 160 + 32 * kl, 0:32] = imag.astype(jnp.bfloat16).astype(jnp.float32) * factor
    else:
        for kl in range(4):
            factor = jnp.where(row_at * 4 + kl == 0, 1.0, 2.0).astype(jnp.float32)
            g_re = modes_ref[pl.ds(kl, 32, stride=8), :][:, :32] * factor
            g_im = modes_ref[pl.ds(4 + kl, 32, stride=8), :][:, :32] * factor

            def one_channel(i, carry):
                s_re = spec_ref[pl.ds(8 * i + kl, 1), :][:, :32]
                s_im = spec_ref[pl.ds(8 * i + 4 + kl, 1), :][:, :32]
                w_re = w_ref[kl, 0, i].astype(jnp.float32)
                w_im = w_ref[kl, 1, i].astype(jnp.float32)
                gspec_ref[kl, 0, i] = g_re * s_re + g_im * s_im
                gspec_ref[kl, 1, i] = g_im * s_re - g_re * s_im
                b_re = jnp.sum(w_re * g_re + w_im * g_im, axis=0, keepdims=True)
                b_im = jnp.sum(w_re * g_im - w_im * g_re, axis=0, keepdims=True)
                mix_ref[pl.ds(32 * kl + i, 1), 0:32] = b_re.astype(jnp.bfloat16).astype(jnp.float32) * scale
                mix_ref[pl.ds(128 + 32 * kl + i, 1), 0:32] = b_im.astype(jnp.bfloat16).astype(jnp.float32) * scale
                return carry

            lax.fori_loop(0, 32, one_channel, 0)

    mix_ref[...] = pltpu.roll(mix_ref[...], quarter, 1)
    for i in range(n_col):
        for odd_channel in range(2):
            upper = mix_ref[pl.ds(4 * i + odd_channel, 8, stride=32), :]
            lower = mix_ref[pl.ds(4 * i + 2 + odd_channel, 8, stride=32), :]
            snd7[i, 16 * odd_channel : 16 * odd_channel + 16] = jnp.concatenate([upper, lower], axis=0).astype(
                jnp.bfloat16
            )
    start7, sent7, got7 = exchange("col", col_at, n_col, lambda i: snd7.at[i], lambda i: rcv7.at[i], s7, r7)
    each(n_col, start7)
    rcv7[col_at] = snd7[col_at]
    each(n_col, got7)
    halves = [sum(rcv7[4 * h + q].astype(jnp.float32) for q in range(4)) for h in range(2)]
    mixed = jnp.concatenate(halves, axis=1)
    swapped = part_swap(mixed, -1.0)
    operand = jnp.concatenate([mixed, swapped], axis=1).astype(jnp.bfloat16)
    by_rows = dot(operand, tx_ref[...], NN)
    for s in range(pairs):
        even = by_rows[0:16, 128 * s : 128 * s + 128]
        odd = by_rows[16:32, 128 * s : 128 * s + 128]
        snd9[2 * s] = jnp.where(low, even, pltpu.roll(odd, 64, 1)).astype(jnp.bfloat16)
        snd9[2 * s + 1] = jnp.where(low, pltpu.roll(even, 64, 1), odd).astype(jnp.bfloat16)
    start9, sent9, got9 = exchange("row", row_at, n_row, lambda i: snd9.at[i], lambda i: rcv9.at[i], s9, r9)
    each(n_row, start9)
    rcv9[row_at] = snd9[row_at]
    each(n_row, got9)
    got = rcv9[...].astype(jnp.float32)
    own_rows = jnp.concatenate(
        [got[:, :8].reshape(8 * n_row, 128), got[:, 8:].reshape(8 * n_row, 128)], axis=1
    )
    lhs = jnp.transpose(own_rows).astype(jnp.bfloat16)
    start10, sent10, got10 = exchange("col", col_at, n_col, lambda i: snd10.at[i], lambda i: rcv10.at[i], s10, r10)

    def make_cells(d):
        peer = lax.rem(col_at + d, n_col)
        snd10[peer] = dot(lhs, ty_ref[peer], NN).astype(jnp.bfloat16)
        start10(d)

    each(n_col, make_cells)
    rcv10[col_at] = dot(lhs, ty_ref[col_at], NN).astype(jnp.bfloat16)
    each(n_col, got10)
    cells_ref[...] = rcv10[...]
    each(n_col, sent1)
    each(n_row, sent3)
    each(n_col, sent5)
    each(n_col, sent7)
    each(n_row, sent9)
    each(n_col, sent10)


def spectral_chain(forward, field, weight, ty, tx, n_row, n_col, spec=None):
    bf16, f32 = (jnp.bfloat16, jnp.float32)
    dma = pltpu.SemaphoreType.DMA
    modes2 = 8 * n_row
    nx = 64 * n_row
    scratch = [
        pltpu.VMEM((n_col, 256, 256), bf16),
        pltpu.VMEM((modes2, 256), f32),
        pltpu.VMEM((n_row, 16, 128), bf16),
        pltpu.VMEM((n_row, 16, 128), bf16),
        pltpu.VMEM((32, nx), bf16),
        pltpu.VMEM((2, 32, 128), bf16),
        pltpu.VMEM((n_col, 32, 128), bf16),
        pltpu.VMEM((256, 128), f32),
        pltpu.VMEM((256, 128), f32),
        pltpu.VMEM((n_col, 32, 128), bf16),
        pltpu.VMEM((n_col, 32, 128), bf16),
        pltpu.VMEM((n_row, 16, 128), bf16),
        pltpu.VMEM((n_row, 16, 128), bf16),
        pltpu.VMEM((n_col, 256, 256), bf16),
        pltpu.VMEM((n_col, 256, 256), bf16),
        dma,
    ]
    for size in (n_col, n_row, n_col, n_col, n_row, n_col):
        scratch += [dma((size,)), dma((size,))]
    vmem = pl.BlockSpec(memory_space=pltpu.VMEM)
    args = [field.reshape(n_col, 256, 256), weight, ty, tx]
    specs = [pl.BlockSpec(memory_space=pl.ANY), vmem, vmem, vmem]
    shapes = [jax.ShapeDtypeStruct((n_col, 256, 256), bf16)]
    if forward:
        shapes.append(jax.ShapeDtypeStruct((256, 128), f32))
    else:
        args.append(spec)
        specs.append(vmem)
        shapes.append(jax.ShapeDtypeStruct(weight.shape, f32))
    cells, other = pl.pallas_call(
        functools.partial(chain_kernel, forward, n_row, n_col),
        out_shape=shapes,
        in_specs=specs,
        out_specs=[vmem, vmem],
        scratch_shapes=scratch,
        compiler_params=pltpu.CompilerParams(
            collective_id=0 if forward else 1, has_side_effects=True, vmem_limit_bytes=VMEM_BYTES
        ),
        name="chain_forward" if forward else "chain_backward",
    )(*args)
    return cells.reshape(field.shape), other


def gelu_parts(pre):
    cdf = 0.5 * (1.0 + jax.scipy.special.erf(pre / math.sqrt(2.0)))
    pdf = jnp.exp(-0.5 * pre * pre) / math.sqrt(TWO_PI)
    return (pre * cdf, cdf + pre * pdf)


def conv_cells(padded, kernel, n_rows, n_cols):
    result = jnp.zeros((kernel.shape[3], n_rows, n_cols), jnp.float32)
    for tap_row in range(3):
        for tap_col in range(3):
            shifted = padded[:, tap_row : tap_row + n_rows, tap_col : tap_col + n_cols]
            result = result + jnp.einsum(
                "io,ixy->oxy", kernel[tap_row, tap_col], shifted, preferred_element_type=jnp.float32
            )
    return result


def conv_transpose(padded, kernel, n_rows, n_cols):
    result = jnp.zeros((kernel.shape[2], n_rows, n_cols), jnp.float32)
    for tap_row in range(3):
        for tap_col in range(3):
            shifted = padded[
                :, 2 - tap_row : 2 - tap_row + n_rows, 2 - tap_col : 2 - tap_col + n_cols
            ]
            result = result + jnp.einsum(
                "io,oxy->ixy", kernel[tap_row, tap_col], shifted, preferred_element_type=jnp.float32
            )
    return result


def kernel_grad(padded, grad_round, n_rows, n_cols):
    taps = []
    for tap_row in range(3):
        for tap_col in range(3):
            shifted = padded[:, tap_row : tap_row + n_rows, tap_col : tap_col + n_cols]
            taps.append(
                jnp.einsum("ixy,oxy->io", shifted, grad_round, preferred_element_type=jnp.float32)
            )
    return jnp.stack(taps).reshape(3, 3, padded.shape[0], grad_round.shape[0])


def per_device(n_row, n_col, ocean_field, cotangent, conv_weight, conv_bias, projection, mode_weight):
    chans, rows_dev, cols_dev = ocean_field.shape
    ky_dev = mode_weight.shape[0]
    kx_all = mode_weight.shape[4] * n_col
    scale = 1.0 / math.sqrt(rows_dev * n_row * cols_dev * n_col)
    ty, tx = (jnp.asarray(t) for t in tables(n_row, n_col, ky_dev, rows_dev, cols_dev, kx_all))

    padded_in = with_halo(ocean_field, (("row", 1), ("col", 2)), 1)
    spectral_cells, spectrum = spectral_chain(True, ocean_field, mode_weight, ty, tx, n_row, n_col)
    pre_act = (
        conv_cells(padded_in, conv_weight, rows_dev, cols_dev)
        + spectral_cells
        + conv_bias[:, None, None]
    )
    activ, slope = gelu_parts(pre_act)
    cot_rows = cotangent.astype(jnp.float32)
    grad_pre = projection[:, None, None] * cot_rows[None] * slope
    grad_round = grad_pre.astype(jnp.bfloat16)
    kernel_part = kernel_grad(padded_in, grad_round, rows_dev, cols_dev)
    bias_part = jnp.sum(grad_pre, axis=(1, 2))
    proj_part = jnp.sum(activ * cot_rows[None], axis=(1, 2))
    kernel_sum, bias_sum, proj_sum = lax.psum((kernel_part, bias_part, proj_part), ("row", "col"))
    padded_grad = with_halo(grad_round, (("row", 1), ("col", 2)), 1)
    spectral_back, grad_spec = spectral_chain(
        False, grad_round, mode_weight, ty, tx, n_row, n_col, spectrum
    )
    back_cells = conv_transpose(padded_grad, conv_weight, rows_dev, cols_dev)
    grad_input = back_cells + spectral_back
    return (grad_input, grad_spec, kernel_sum * scale, bias_sum * scale, proj_sum * scale)


def solution(mesh):
    placed = (
        P(None, "row", "col"),
        P("row", "col"),
        P(),
        P(),
        P(),
        P("row", None, None, None, "col"),
    )
    return jax.shard_map(
        functools.partial(per_device, mesh.shape["row"], mesh.shape["col"]),
        mesh=mesh,
        in_specs=placed,
        out_specs=(P(None, "row", "col"), P("row", None, None, None, "col"), P(), P(), P()),
        check_vma=False,
    )
```

time: 577 us -> 318 us (0.55); the launches traced: 568 us -> 317 us
  waiting for transfers between devices: 190 us -> 0.02 us
  Pallas kernels: 0 us -> 140 us
  blocking collectives: 157 us -> 80.3 us
  matrix products: 81.5 us -> 37.2 us
  starting transfers between devices: 51.6 us -> 22 us
  local copies, waits for them, and re-layouts: 47.8 us -> 26.3 us
  other arithmetic: 25.1 us -> 10.1 us
  between operations: 15.5 us -> 1.07 us
    pallas_call x0 -> x2, Pallas kernels: none -> 140 us  [spectral_chain(): pl.pallas_call(functools.partial(chain_kernel, forward, n_row, n_col), ou...]
    reduce_scatter x2 -> x0, waiting for transfers between devices: 101 us -> none  [column_sums(): lax.psum_scatter(partial_value, 'col', scatter_dimension=3, tiled=True)]
    all_gather x2 -> x0, blocking collectives: 48.2 us -> none  [to_grid(): pieces = lax.all_gather(spectral, 'col', axis=3, tiled=True)]
    all_to_all x1 -> x0, blocking collectives: 33.7 us -> none  [to_grid(): lax.all_to_all(summed, 'row', split_axis=3, concat_axis=0, tiled=True)]
    all_to_all x3 -> x0, waiting for transfers between devices: 32.2 us -> none  [the longest x2 21.8 us: forward_modes(): lax.all_to_all(whole_y, 'row', split_axis=0, concat_axis=3, tiled=True)]
    all_to_all x3 -> x0, starting transfers between devices: 30.1 us -> none  [the longest x2 19.1 us: forward_modes(): lax.all_to_all(whole_y, 'row', split_axis=0, concat_axis=3, tiled=True)]
    unnamed x8 -> x0, waiting for transfers between devices: 28.6 us -> none
    all_gather x2 -> x0, waiting for transfers between devices: 27.5 us -> none  [to_grid(): lax.all_gather(returned, 'col', axis=3, tiled=True)]
  transfers between devices with their start and end apart: 17 -> 8, of which waited for: 8 -> 0; matrix products, arithmetic and copies ran while one was open for 17% -> 11% of each run, Pallas kernels for 0% -> 44%
where the time goes in v1:
time: 318 us; the launch traced here: 317 us
  Pallas kernels  140 us (44%)
  blocking collectives  80.3 us (25%)
  matrix products  37.2 us (12%)
  local copies, waits for them, and re-layouts  26.3 us (8%)
  starting transfers between devices  22 us (7%)
  other arithmetic  10.1 us (3%)
    pallas_call x2, Pallas kernels, spectral_chain(): pl.pallas_call(functools.partial(chain_kernel, forward, n_row, n_col), ou...  140 us
    psum x1, blocking collectives, per_device(): lax.psum((kernel_part, bias_part, proj_part), ('row', 'col'))  80.3 us
    dot_general x9, matrix products, conv_cells(): jnp.einsum('io,ixy->oxy', kernel[tap_row, tap_col], shifted, preferred_el...  22.1 us
    ppermute x4, starting transfers between devices, with_halo(): after = lax.ppermute(first, axis, down)  11 us
    ppermute x4, starting transfers between devices, with_halo(): before = lax.ppermute(last, axis, up)  11 us
    unnamed x47, local copies, waits for them, and re-layouts  10.9 us
    dot_general x9, matrix products, conv_transpose(): jnp.einsum('io,oxy->ixy', kernel[tap_row, tap_col], shifted, preferred_el...  9.86 us
  transfers between devices with their start and end apart: 8, of which 0 were waited for; matrix products, arithmetic and copies ran while one was open for 11% of the time, Pallas kernels for 44%

profile of v1, /device:TPU:1, one launch (start us, length us, event | category | flops | bytes accessed | tf_op | source)
XLA Modules:
  0.0 316.9 jit_solution(6337562574937426076)
XLA Ops:
  0.6 1.0 fusion.110
  1.7 5.1 %collective-permute-start.1 = (bf16[32,1,256]{2,0,1:T(8,128)(2,1)S(1)}, bf16[32,1,256]{2,0,1:T(8,128)(2,1)S(1)}, u32[]{:S(2)}, u32[]{:S(2)}) collective-permute-start(bf16[32,1,256]{2,0,1:T(8,128)(2,1)S(1)} %copy.119), channel_id=1, source_target_pairs={{8,0},{16,8},{24,16},{32,24},{40,32},{48,40},{56,48},{64,56},{72,6... | collective-permute-start | bytes 49160 | tf_op jit(solution)/shard_map/ppermute | solution.py:25
  6.9 1.9 collective-permute-start
  8.8 3.3 %fusion.58 = f32[32,64,256]{2,0,1:T(8,128)} fusion(bf16[3,3,32,32]{3,2,1,0:T(8,128)(2,1)} %param.10, bf16[32,64,256]{2,1,0:T(8,128)(2,1)} %param.8), kind=kOutput, calls=%fused_computation.95 | convolution fusion | flops 33554432 | bytes 3153920 | tf_op jit(solution)/shard_map/io,ixy->oxy/dot_general | solution.py:307
  12.1 72.3 %chain_forward.1 = (bf16[8,256,256]{2,1,0:T(8,128)(2,1)}, f32[256,128]{1,0:T(8,128)}) custom-call(bf16[8,256,256]{2,1,0:T(8,128)(2,1)} %bitcast.183, bf16[4,2,32,32,32]{4,3,2,1,0:T(8,128)(2,1)} %refs_1_.3, bf16[8,256,256]{2,1,0:T(8,128)(2,1)} %constant.21.clone.refs_2_, bf16[512,2048]{1,0:T(8,128)(2,1)} %constant.22.clone.refs_3_), custom_call_target="tpu_custom_call" | custom-call | tf_op jit(solution)/shard_map/chain_forward/pallas_call | solution.py:282
  84.5 2.9 convert.2
  88.1 1.0 copy-done.1
  89.4 1.1 fusion.108
  90.5 1.7 copy.51
  92.1 0.7 copy.46
  92.8 1.9 collective-permute-start.2
  94.7 1.5 collective-permute-start.3
  96.2 3.0 fusion.42
  99.2 3.0 fusion.44
  102.2 0.9 copy.47
  103.2 1.9 fusion.46
  105.1 1.9 fusion.69
  107.0 1.9 fusion.61
  108.9 0.9 copy.52
  112.3 0.8 copy-done.11
  113.1 5.7 %multiply_reduce_fusion = (f32[32]{0:T(128)S(1)}, f32[32]{0:T(128)S(1)}, f32[32,64,256]{2,0,1:T(8,128)S(1)}, f32[32,64,256]{2,0,1:T(8,128)S(1)}) fusion(f32[64,256]{1,0:T(8,128)S(1)} %convert_element_type.18, f32[32]{0:T(128)S(1)} %copy-done.19, f32[32]{0:T(128)S(1)} %copy-done.20, f32[32,64,256]{2,1,0:T(8,128)} %convert.2, ...), kind=kOutput, calls=%fused_computation.14 | convolution fusion | flops 48234432 | bytes 24765696 | tf_op jit(solution)/shard_map/io,ixy->oxy/dot_general | solution.py:307
  118.8 0.7 fusion.104
  120.4 1.8 fusion.56
  122.2 3.1 collective-permute-start.5
  125.3 2.9 collective-permute-start.4
  128.7 0.7 fusion.14
  129.9 0.8 fusion.12
  132.0 0.7 copy-done.2
  133.8 80.3 %all-reduce = (f32[3,3,32,32]{3,2,1,0:T(8,128)S(1)}, f32[32]{0:T(128)S(1)}, f32[32]{0:T(128)S(1)}) all-reduce(f32[3,3,32,32]{3,2,1,0:T(8,128)S(1)} %bitcast.187, f32[32]{0:T(128)S(1)} %get-tuple-element.24, f32[32]{0:T(128)S(1)} %get-tuple-element.23), channel_id=1, replica_groups=mesh['row'=32,'col'=8] {'row','col'}, use_global_device_ids=true, to_apply=%region_0.0 | all-reduce | flops 9280 | bytes 74240 | tf_op jit(solution)/shard_map/psum | solution.py:358
  214.1 0.7 broadcast_multiply_fusion
  215.2 1.6 copy.76
  216.8 67.6 %chain_backward.1 = (bf16[8,256,256]{2,1,0:T(8,128)(2,1)}, f32[4,2,32,32,32]{4,3,2,1,0:T(8,128)}) custom-call(bf16[8,256,256]{2,1,0:T(8,128)(2,1)} %bitcast.184, bf16[4,2,32,32,32]{4,3,2,1,0:T(8,128)(2,1)} %refs_1_.3, bf16[8,256,256]{2,1,0:T(8,128)(2,1)} %constant.21.clone.refs_2_, bf16[512,2048]{1,0:T(8,128)(2,1)} %constant.22.clone.refs_3_, ...), custom_call_target="tpu_custom_call" | custom-call | tf_op jit(solution)/shard_map/chain_backward/pallas_call | solution.py:282
  284.4 2.8 convert.3
  287.3 1.1 fusion.107
  288.4 1.7 copy.67
  290.0 0.7 copy.63
  290.7 1.3 collective-permute-start.6
  292.0 4.2 %collective-permute-start.7 = (bf16[32,66,1]{1,0,2:T(8,128)(2,1)S(1)}, bf16[32,66,1]{1,0,2:T(8,128)(2,1)S(1)}, u32[]{:S(2)}, u32[]{:S(2)}) collective-permute-start(bf16[32,66,1]{1,0,2:T(8,128)(2,1)S(1)} %copy.67), channel_id=1, source_target_pairs={{0,1},{1,2},{2,3},{3,4},{4,5},{5,6},{6,7},{8,9},{9,10},{10,11},{11... | collective-permute-start | bytes 12680 | tf_op jit(solution)/shard_map/ppermute | solution.py:24
  296.3 1.7 fusion.20
  298.0 1.8 fusion.16
  299.8 1.8 copy.68
  301.6 1.7 copy.64
  303.3 2.4 maximum_maximum_fusion
  308.1 0.8 copy-done.8
  309.5 0.7 copy-done.7
  310.2 2.2 bitcast_add_fusion
  312.4 2.5 copy.80
  314.9 2.0 copy.134
  (68 shorter events, 11.2 us)
Async XLA Ops:
  0.6 11.5 %copy-start.18 = (bf16[64,256]{1,0:T(8,128)(2,1)S(1)}, bf16[64,256]{1,0:T(8,128)(2,1)}, u32[]{:S(2)}) copy-start(bf16[64,256]{1,0:T(8,128)(2,1)} %param.9) | copy-start | bytes 98308
  1.7 86.4 %collective-permute-start.1 = (bf16[32,1,256]{2,0,1:T(8,128)(2,1)S(1)}, bf16[32,1,256]{2,0,1:T(8,128)(2,1)S(1)}, u32[]{:S(2)}, u32[]{:S(2)}) collective-permute-start(bf16[32,1,256]{2,0,1:T(8,128)(2,1)S(1)} %copy.119), channel_id=1, source_target_pairs={{8,0},{16,8},{24,16},{32,24},{40,32},{48,40},{56,48},{64,56},{72,6... | collective-permute-start | bytes 49160 | tf_op jit(solution)/shard_map/ppermute | solution.py:25
  6.9 80.5 %collective-permute-start = (bf16[32,1,256]{2,0,1:T(8,128)(2,1)S(1)}, bf16[32,1,256]{2,0,1:T(8,128)(2,1)S(1)}, u32[]{:S(2)}, u32[]{:S(2)}) collective-permute-start(bf16[32,1,256]{2,0,1:T(8,128)(2,1)S(1)} %copy.120), channel_id=1, source_target_pairs={{0,8},{8,16},{16,24},{24,32},{32,40},{40,48},{48,56},{56,64},{64,7... | collective-permute-start | bytes 49160 | tf_op jit(solution)/shard_map/ppermute | solution.py:24
  84.5 2.9 copy-start
  88.1 1.4 copy-start.14
  88.1 8.1 %copy-start.17 = (bf16[3,3,32,32]{3,2,1,0:T(8,128)(2,1)S(1)}, bf16[3,3,32,32]{3,2,1,0:T(8,128)(2,1)}, u32[]{:S(2)}) copy-start(bf16[3,3,32,32]{3,2,1,0:T(8,128)(2,1)} %param.10) | copy-start | bytes 55300
  88.1 1.0 copy-start.1
  92.8 9.4 %collective-permute-start.2 = (bf16[32,66,1]{1,0,2:T(8,128)(2,1)S(1)}, bf16[32,66,1]{1,0,2:T(8,128)(2,1)S(1)}, u32[]{:S(2)}, u32[]{:S(2)}) collective-permute-start(bf16[32,66,1]{1,0,2:T(8,128)(2,1)S(1)} %copy.46), channel_id=1, source_target_pairs={{0,1},{1,2},{2,3},{3,4},{4,5},{5,6},{6,7},{8,9},{9,10},{10,11},{11... | collective-permute-start | bytes 12680 | tf_op jit(solution)/shard_map/ppermute | solution.py:24
  94.7 14.2 %collective-permute-start.3 = (bf16[32,66,1]{1,0,2:T(8,128)(2,1)S(1)}, bf16[32,66,1]{1,0,2:T(8,128)(2,1)S(1)}, u32[]{:S(2)}, u32[]{:S(2)}) collective-permute-start(bf16[32,66,1]{1,0,2:T(8,128)(2,1)S(1)} %copy.51), channel_id=1, source_target_pairs={{1,0},{2,1},{3,2},{4,3},{5,4},{6,5},{7,6},{9,8},{10,9},{11,10},{12... | collective-permute-start | bytes 12680 | tf_op jit(solution)/shard_map/ppermute | solution.py:25
  103.2 3.8 %copy-start.3 = (bf16[32,66,1]{2,0,1:T(8,128)(2,1)}, bf16[32,66,1]{2,0,1:T(8,128)(2,1)S(1)}, u32[]{:S(2)}) copy-start(bf16[32,66,1]{2,0,1:T(8,128)(2,1)S(1)} %copy.47) | copy-start | bytes 12676
  109.9 1.4 copy-start.5
  109.9 1.8 copy-start.12
  109.9 2.4 copy-start.13
  110.6 2.5 copy-start.11
  110.6 2.5 copy-start.19
  110.6 2.5 copy-start.20
  118.8 1.0 copy-start.4
  120.3 7.9 %copy-start.15 = (bf16[32,65,256]{2,0,1:T(8,128)(2,1)S(1)}, bf16[32,65,256]{2,0,1:T(8,128)(2,1)}, u32[]{:S(2)}) copy-start(bf16[32,65,256]{2,0,1:T(8,128)(2,1)} %copy-done.14) | copy-start | bytes 3194884
  120.3 8.3 %copy-start.6 = (bf16[32,66,1]{2,0,1:T(8,128)(2,1)S(1)}, bf16[32,66,1]{2,0,1:T(8,128)(2,1)}, u32[]{:S(2)}) copy-start(bf16[32,66,1]{2,0,1:T(8,128)(2,1)} %copy-done.5) | copy-start | bytes 12676
  122.2 165.0 %collective-permute-start.5 = (bf16[32,1,256]{2,0,1:T(8,128)(2,1)S(1)}, bf16[32,1,256]{2,0,1:T(8,128)(2,1)S(1)}, u32[]{:S(2)}, u32[]{:S(2)}) collective-permute-start(bf16[32,1,256]{2,0,1:T(8,128)(2,1)S(1)} %get-tuple-element.35), channel_id=1, source_target_pairs={{8,0},{16,8},{24,16},{32,24},{40,32},{48,40},{56,48},{64,56},{72,6... | collective-permute-start | bytes 49160 | tf_op jit(solution)/shard_map/ppermute | solution.py:25
  125.3 161.9 %collective-permute-start.4 = (bf16[32,1,256]{2,0,1:T(8,128)(2,1)S(1)}, bf16[32,1,256]{2,0,1:T(8,128)(2,1)S(1)}, u32[]{:S(2)}, u32[]{:S(2)}) collective-permute-start(bf16[32,1,256]{2,0,1:T(8,128)(2,1)S(1)} %get-tuple-element.36), channel_id=1, source_target_pairs={{0,8},{8,16},{16,24},{24,32},{32,40},{40,48},{48,56},{56,64},{64,7... | collective-permute-start | bytes 49160 | tf_op jit(solution)/shard_map/ppermute | solution.py:24
  131.4 1.3 copy-start.2
  290.7 10.9 %collective-permute-start.6 = (bf16[32,66,1]{1,0,2:T(8,128)(2,1)S(1)}, bf16[32,66,1]{1,0,2:T(8,128)(2,1)S(1)}, u32[]{:S(2)}, u32[]{:S(2)}) collective-permute-start(bf16[32,66,1]{1,0,2:T(8,128)(2,1)S(1)} %copy.63), channel_id=1, source_target_pairs={{1,0},{2,1},{3,2},{4,3},{5,4},{6,5},{7,6},{9,8},{10,9},{11,10},{12... | collective-permute-start | bytes 12680 | tf_op jit(solution)/shard_map/ppermute | solution.py:25
  292.0 7.8 %collective-permute-start.7 = (bf16[32,66,1]{1,0,2:T(8,128)(2,1)S(1)}, bf16[32,66,1]{1,0,2:T(8,128)(2,1)S(1)}, u32[]{:S(2)}, u32[]{:S(2)}) collective-permute-start(bf16[32,66,1]{1,0,2:T(8,128)(2,1)S(1)} %copy.67), channel_id=1, source_target_pairs={{0,1},{1,2},{2,3},{3,4},{4,5},{5,6},{6,7},{8,9},{9,10},{10,11},{11... | collective-permute-start | bytes 12680 | tf_op jit(solution)/shard_map/ppermute | solution.py:24
  306.5 1.6 copy-start.10
  307.0 1.8 copy-start.8
  307.0 2.5 copy-start.9
  307.6 2.6 copy-start.7
  312.4 2.5 copy-start.16

commit v2 on v1

v2 whole, which is shorter than its diff:
```python
import functools
import math

import jax
import jax.numpy as jnp
import ml_dtypes
import numpy as np
from jax import lax
from jax.experimental import pallas as pl
from jax.experimental.pallas import tpu as pltpu
from jax.sharding import PartitionSpec as P

TWO_PI = 2.0 * math.pi
HIGH = lax.Precision.HIGHEST
VMEM_BYTES = 56 * 1024 * 1024


def angle_pair(products, period):
    angles = (products % period).astype(np.float32) * np.float32(TWO_PI / period)
    return (np.cos(angles).astype(ml_dtypes.bfloat16), np.sin(angles).astype(ml_dtypes.bfloat16))


def tables(n_row, n_col, ky_dev, rows_dev, cols_dev, kx_all):
    modes, nx, ny = (ky_dev * n_row, rows_dev * n_row, cols_dev * n_col)
    cosine, sine = angle_pair(np.arange(modes)[:, None] * np.arange(ny)[None, :], ny)
    ty = np.stack([cosine.reshape(n_row, ky_dev, ny), -sine.reshape(n_row, ky_dev, ny)], axis=1)
    ty = ty.reshape(2 * modes, n_col, cols_dev).transpose(1, 0, 2)
    ids = np.arange(kx_all)
    freqs = np.where(ids < modes, ids, ids - 2 * modes) % nx
    cosine, sine = angle_pair(freqs[:, None] * np.arange(nx)[None, :], nx)
    return np.ascontiguousarray(ty), np.concatenate([cosine, sine], axis=0)


NT = (((1,), (1,)), ((), ()))
NN = (((1,), (0,)), ((), ()))
TN = (((0,), (0,)), ((), ()))


def dot(a, b, dims):
    return lax.dot_general(a, b, dims, preferred_element_type=jnp.float32)


def exchange(axis, me, size, source, target, send_sem, recv_sem):
    def copy(step, peer, slot):
        return pltpu.make_async_remote_copy(
            src_ref=source(peer),
            dst_ref=target(slot),
            send_sem=send_sem.at[step],
            recv_sem=recv_sem.at[step],
            device_id={axis: peer},
            device_id_type=pl.DeviceIdType.MESH,
        )

    def start(step):
        copy(step, lax.rem(me + step, size), me).start()

    def wait_send(step):
        copy(step, lax.rem(me + step, size), me).wait_send()

    def wait_recv(step):
        origin = lax.rem(me + size - step, size)
        copy(step, lax.rem(me + step, size), origin).wait_recv()
        return origin

    return start, wait_send, wait_recv


def each(size, body):
    def step(index, carry):
        body(index)
        return carry

    lax.fori_loop(1, size, step, 0)


def part_swap(value, sign):
    rows = value.shape[0]
    is_real = (lax.broadcasted_iota(jnp.int32, value.shape, 0) & 4) == 0
    after = pltpu.roll(value, rows - 4, 0)
    before = pltpu.roll(value, 4, 0)
    return jnp.where(is_real, sign * after, -sign * before)


class Group:
    def __init__(self, names, refs):
        for name, ref in zip(names, refs):
            setattr(self, name, ref)


def push(src, dst, send_sem, recv_sem, axis, peer):
    return pltpu.make_async_remote_copy(
        src_ref=src,
        dst_ref=dst,
        send_sem=send_sem,
        recv_sem=recv_sem,
        device_id={axis: peer},
        device_id_type=pl.DeviceIdType.MESH,
    )


def aligned(value, to):
    return pl.multiple_of(value, to)


def pass_scratch(n_row, n_col):
    bf16, f32 = (jnp.bfloat16, jnp.float32)
    dma = pltpu.SemaphoreType.DMA
    found = dict(
        snd1=pltpu.VMEM((n_col, 256, 256), bf16),
        buf1=pltpu.VMEM((n_col, 256, 256), bf16),
        snd3=pltpu.VMEM((n_row, 16, 128), bf16),
        rcv3=pltpu.VMEM((n_row, 16, 128), bf16),
        snd5=pltpu.VMEM((2, 32, 128), bf16),
        rcv5=pltpu.VMEM((n_col, 32, 128), bf16),
        modes=pltpu.VMEM((256, 128), f32),
        snd7=pltpu.VMEM((n_col, 32, 128), bf16),
        rcv7=pltpu.VMEM((n_col, 32, 128), bf16),
        snd9=pltpu.VMEM((n_row, 16, 128), bf16),
        rcv9=pltpu.VMEM((n_row, 16, 128), bf16),
        snd10=pltpu.VMEM((n_col, 256, 256), bf16),
        rcv10=pltpu.VMEM((n_col, 256, 256), bf16),
        raw=pltpu.VMEM((68 * 32, 256), bf16),
        halo=pltpu.VMEM((2, 32, 256), bf16),
        edge_out=pltpu.VMEM((2, 16, 68 * 32), bf16),
        edge_in=pltpu.VMEM((2, 16, 68 * 32), bf16),
        wide=pltpu.VMEM((68 * 96, 256), bf16),
        taps=pltpu.VMEM((256, 1024), bf16),
        own=dma,
        hs=dma((2,)),
        hr=dma((2,)),
        es=dma((2,)),
        er=dma((2,)),
    )
    for step, size in ((1, n_col), (3, n_row), (5, n_col), (7, n_col), (9, n_row), (10, n_col)):
        found["s%d" % step] = dma((size,))
        found["r%d" % step] = dma((size,))
    return found


def common_scratch(n_row, n_col, nx, owners):
    bf16, f32 = (jnp.bfloat16, jnp.float32)
    dma = pltpu.SemaphoreType.DMA
    piece = 80 // owners
    return dict(
        vbuf=pltpu.VMEM((n_col, 256, 256), bf16),
        ty=pltpu.VMEM((n_col, 8 * n_row, 256), bf16),
        tx=pltpu.VMEM((512, nx), bf16),
        weight=pltpu.VMEM((4, 2, 32, 32, 32), bf16),
        stage=pltpu.VMEM((4096, 128), f32),
        cells=pltpu.VMEM((2048, 256), f32),
        cot=pltpu.VMEM((64, 256), f32),
        acc=pltpu.VMEM((8 * n_row, 256), f32),
        rows_x=pltpu.VMEM((32, nx), bf16),
        mix=pltpu.VMEM((256, 128), f32),
        outer=pltpu.VMEM((960, 256), f32),
        sums=pltpu.VMEM((128, 256), f32),
        part=pltpu.VMEM((owners, piece, 128), f32),
        got_row=pltpu.VMEM((n_row, piece, 128), f32),
        sum_row=pltpu.VMEM((piece, 128), f32),
        got_col=pltpu.VMEM((n_col, piece, 128), f32),
        total=pltpu.VMEM((piece, 128), f32),
        got_all=pltpu.VMEM((owners, piece, 128), f32),
        load=dma((4,)),
        row_s=dma((owners,)),
        row_r=dma((n_row,)),
        col_s=dma((n_col,)),
        col_r=dma((n_col,)),
        all_s=dma((n_row,)),
        all_r=dma((owners,)),
    )


def step_kernel(n_row, n_col, owners, *refs):
    (v_ref, cot_ref, w2_ref, bias_ref, proj_ref, w_hbm, ty_hbm, tx_hbm, out_ref, gspec_ref, small_ref, *rest) = refs
    nx = 64 * n_row
    names = list(pass_scratch(n_row, n_col))
    first = Group(names, rest[: len(names)])
    second = Group(names, rest[len(names) : 2 * len(names)])
    g = Group(list(common_scratch(n_row, n_col, nx, owners)), rest[2 * len(names) :])
    row_at = lax.axis_index("row")
    col_at = lax.axis_index("col")
    pairs = n_row // 2
    scale = 1.0 / math.sqrt((64 * n_row) * (256 * n_col))
    bf16, f32 = (jnp.bfloat16, jnp.float32)
    pending = []

    loads = [
        pltpu.make_async_copy(v_ref, g.vbuf, g.load.at[0]),
        pltpu.make_async_copy(ty_hbm, g.ty, g.load.at[1]),
        pltpu.make_async_copy(tx_hbm, g.tx, g.load.at[2]),
        pltpu.make_async_copy(w_hbm, g.weight, g.load.at[3]),
    ]
    for load in loads:
        load.start()
    barrier = pltpu.get_barrier_semaphore()
    each(n_col, lambda d: pl.semaphore_signal(
        barrier, inc=1, device_id={"col": lax.rem(col_at + d, n_col)}, device_id_type=pl.DeviceIdType.MESH))
    each(n_row, lambda d: pl.semaphore_signal(
        barrier, inc=1, device_id={"row": lax.rem(row_at + d, n_row)}, device_id_type=pl.DeviceIdType.MESH))
    pl.semaphore_wait(barrier, n_col - 1 + n_row - 1)

    def loop(size, body):
        def step(index, carry):
            body(index)
            return carry

        lax.fori_loop(0, size, step, 0)

    def send_halo_rows(p):
        up = lax.rem(row_at + n_row - 1, n_row)
        down = lax.rem(row_at + 1, n_row)
        copies = [
            push(p.raw.at[pl.ds(32, 32)], p.halo.at[1], p.hs.at[0], p.hr.at[0], "row", up),
            push(p.raw.at[pl.ds(64 * 32, 32)], p.halo.at[0], p.hs.at[1], p.hr.at[1], "row", down),
        ]
        for copy in copies:
            copy.start()
            pending.append(copy.wait_send)
        return copies

    def widen(p, row_copies):
        for copy in row_copies:
            copy.wait_recv()
        above = jnp.where(row_at > 0, 1.0, 0.0)
        below = jnp.where(row_at < n_row - 1, 1.0, 0.0)
        p.raw[0:32] = (p.halo[0].astype(f32) * above).astype(bf16)
        p.raw[65 * 32 : 66 * 32] = (p.halo[1].astype(f32) * below).astype(bf16)
        p.raw[66 * 32 : 68 * 32] = jnp.zeros((64, 256), bf16)
        row = lax.broadcasted_iota(jnp.int32, (32, 256), 0)
        lane = lax.broadcasted_iota(jnp.int32, (32, 256), 1)
        pick = ((row == 0) & (lane == 0)) | ((row == 16) & (lane == 255))
        edges = dot(jnp.where(pick, 1.0, 0.0).astype(bf16), p.raw[...], NT)
        p.edge_out[0] = edges[0:16].astype(bf16)
        p.edge_out[1] = edges[16:32].astype(bf16)
        left = lax.rem(col_at + n_col - 1, n_col)
        right = lax.rem(col_at + 1, n_col)
        copies = [
            push(p.edge_out.at[0], p.edge_in.at[1], p.es.at[0], p.er.at[0], "col", left),
            push(p.edge_out.at[1], p.edge_in.at[0], p.es.at[1], p.er.at[1], "col", right),
        ]
        for copy in copies:
            copy.start()
            pending.append(copy.wait_send)
        return copies

    def fill_wide(p, copies):
        for copy in copies:
            copy.wait_recv()
        row = lax.broadcasted_iota(jnp.int32, (16, 128), 0)
        lane = lax.broadcasted_iota(jnp.int32, (16, 128), 1)
        put_left = jnp.where((row == 0) & (lane == 0) & (col_at > 0), 1.0, 0.0).astype(bf16)
        put_right = jnp.where((row == 0) & (lane == 127) & (col_at < n_col - 1), 1.0, 0.0).astype(bf16)
        lanes = lax.broadcasted_iota(jnp.int32, (128, 128), 1)

        def chunk(q):
            here = p.raw[pl.ds(aligned(q * 128, 128), 128), :].astype(f32)
            from_left = dot(p.edge_in[0, :, pl.ds(aligned(q * 128, 128), 128)], put_left, TN)
            from_right = dot(p.edge_in[1, :, pl.ds(aligned(q * 128, 128), 128)], put_right, TN)
            before = pltpu.roll(here, 1, 1)
            after = pltpu.roll(here, 255, 1)
            before = jnp.concatenate([jnp.where(lanes == 0, from_left, before[:, :128]), before[:, 128:]], axis=1)
            after = jnp.concatenate([after[:, :128], jnp.where(lanes == 127, from_right, after[:, 128:])], axis=1)
            for x in range(4):
                for b, value in enumerate((before, here, after)):
                    base = aligned(q * 384 + 96 * x + 32 * b, 32)
                    p.wide[pl.ds(base, 32), :] = value[32 * x : 32 * x + 32].astype(bf16)

        loop(17, chunk)

    def convolve(p, kernel):
        padded = w2_ref[kernel]
        for x in range(8):
            p.taps[32 * x : 32 * x + 32, :] = (pltpu.roll(padded, 96 * x, 1) if x else padded).astype(bf16)

        def block(t):
            rows = p.wide[pl.ds(aligned(t * 768, 16), 1024), :]
            g.cells[pl.ds(aligned(t * 256, 256), 256), :] = dot(p.taps[...], rows, NN)

        loop(8, block)

    def to_modes(p, source, cover, cover_rows):
        own = pltpu.make_async_copy(source(col_at), p.buf1.at[col_at], p.own)
        own.start()
        start, sent, got = exchange("col", col_at, n_col, source, lambda i: p.buf1.at[i], p.s1, p.r1)
        each(n_col, start)
        pending.append(lambda: each(n_col, sent))
        cover()
        own.wait()
        g.acc[...] = dot(g.ty[col_at], p.buf1[col_at], NT)

        def add_block(d):
            origin = got(d)
            g.acc[...] += dot(g.ty[origin], p.buf1[origin], NT)

        each(n_col, add_block)
        whole = g.acc[...]
        upper = whole[:, :128].reshape(n_row, 8, 128)
        lower = whole[:, 128:].reshape(n_row, 8, 128)
        p.snd3[...] = jnp.concatenate([upper, lower], axis=1).astype(bf16)
        start3, sent3, got3 = exchange("row", row_at, n_row, lambda i: p.snd3.at[i], lambda i: p.rcv3.at[i], p.s3, p.r3)
        each(n_row, start3)
        pending.append(lambda: each(n_row, sent3))
        p.rcv3[row_at] = p.snd3[row_at]
        cover_rows()
        each(n_row, got3)
        for s in range(pairs):
            one = p.rcv3[2 * s].astype(f32)
            two = p.rcv3[2 * s + 1].astype(f32)
            even = jnp.where(low, one, pltpu.roll(two, 64, 1))
            odd = jnp.where(low, pltpu.roll(one, 64, 1), two)
            g.rows_x[0:16, 128 * s : 128 * s + 128] = even.astype(bf16)
            g.rows_x[16:32, 128 * s : 128 * s + 128] = odd.astype(bf16)
        both = dot(g.rows_x[...], g.tx[...], NT)
        coeffs = (both[:, :256] + part_swap(both[:, 256:], 1.0)) * scale
        coeffs = jnp.concatenate([coeffs[0:8], coeffs[16:24], coeffs[8:16], coeffs[24:32]], axis=0)
        p.snd5[0] = coeffs[:, :128].astype(bf16)
        p.snd5[1] = coeffs[:, 128:].astype(bf16)
        start5, sent5, got5 = exchange(
            "col", col_at, n_col, lambda i: p.snd5.at[i // 4], lambda i: p.rcv5.at[i], p.s5, p.r5
        )
        each(n_col, start5)
        pending.append(lambda: each(n_col, sent5))
        p.rcv5[col_at] = p.snd5[col_at // 4]
        g.mix[...] = jnp.zeros_like(g.mix)
        each(n_col, got5)
        for i in range(n_col):
            p.modes[32 * i : 32 * i + 32] = pltpu.roll(p.rcv5[i].astype(f32), back_shift, 1)

    def to_grid(p, cover_rows):
        g.mix[...] = pltpu.roll(g.mix[...], quarter, 1)
        for i in range(n_col):
            for odd_channel in range(2):
                upper = g.mix[pl.ds(4 * i + odd_channel, 8, stride=32), :]
                lower = g.mix[pl.ds(4 * i + 2 + odd_channel, 8, stride=32), :]
                p.snd7[i, 16 * odd_channel : 16 * odd_channel + 16] = jnp.concatenate(
                    [upper, lower], axis=0
                ).astype(bf16)
        start7, sent7, got7 = exchange("col", col_at, n_col, lambda i: p.snd7.at[i], lambda i: p.rcv7.at[i], p.s7, p.r7)
        each(n_col, start7)
        pending.append(lambda: each(n_col, sent7))
        p.rcv7[col_at] = p.snd7[col_at]
        each(n_col, got7)
        halves = [sum(p.rcv7[4 * h + q].astype(f32) for q in range(4)) for h in range(2)]
        mixed = jnp.concatenate(halves, axis=1)
        swapped = part_swap(mixed, -1.0)
        operand = jnp.concatenate([mixed, swapped], axis=1).astype(bf16)
        by_rows = dot(operand, g.tx[...], NN)
        for s in range(pairs):
            even = by_rows[0:16, 128 * s : 128 * s + 128]
            odd = by_rows[16:32, 128 * s : 128 * s + 128]
            p.snd9[2 * s] = jnp.where(low, even, pltpu.roll(odd, 64, 1)).astype(bf16)
            p.snd9[2 * s + 1] = jnp.where(low, pltpu.roll(even, 64, 1), odd).astype(bf16)
        start9, sent9, got9 = exchange("row", row_at, n_row, lambda i: p.snd9.at[i], lambda i: p.rcv9.at[i], p.s9, p.r9)
        each(n_row, start9)
        pending.append(lambda: each(n_row, sent9))
        p.rcv9[row_at] = p.snd9[row_at]
        cover_rows()
        each(n_row, got9)
        got = p.rcv9[...].astype(f32)
        own_rows = jnp.concatenate(
            [got[:, :8].reshape(8 * n_row, 128), got[:, 8:].reshape(8 * n_row, 128)], axis=1
        )
        lhs = jnp.transpose(own_rows).astype(bf16)
        start10, sent10, got10 = exchange(
            "col", col_at, n_col, lambda i: p.snd10.at[i], lambda i: p.rcv10.at[i], p.s10, p.r10
        )

        def make_cells(d):
            peer = lax.rem(col_at + d, n_col)
            p.snd10[peer] = dot(lhs, g.ty[peer], NN).astype(bf16)
            start10(d)

        each(n_col, make_cells)
        pending.append(lambda: each(n_col, sent10))

        place(col_at, dot(lhs, g.ty[col_at], NN))

        def take(d):
            origin = got10(d)
            place(origin, p.rcv10[origin].astype(f32))

        each(n_col, take)

    def nothing():
        return None

    def place(slot, value):
        for half in range(2):
            g.stage[pl.ds(aligned(half * 2048 + slot * 256, 256), 256), :] = value[:, 128 * half : 128 * half + 128]

    def placed(slot):
        return jnp.concatenate(
            [g.stage[2048 * half + 256 * slot : 2048 * half + 256 * slot + 256] for half in range(2)], axis=1
        )

    def grid_row(x):
        return jnp.concatenate([g.stage[pl.ds(2048 * half + x, 32, stride=64), :] for half in range(2)], axis=1)

    def put_grid_row(x, value):
        for half in range(2):
            g.stage[pl.ds(2048 * half + x, 32, stride=64), :] = value[:, 128 * half : 128 * half + 128]

    low = lax.broadcasted_iota(jnp.int32, (16, 128), 1) < 64
    quarter = lax.rem(col_at, 4) * 32
    back_shift = lax.rem(128 - quarter, 128)

    def cover_field():
        loads[0].wait()
        for i in range(n_col):
            place(i, g.vbuf[i].astype(f32))

        def regroup(x):
            first.raw[pl.ds(aligned(x * 32 + 32, 32), 32), :] = grid_row(x).astype(bf16)

        regroup(0)
        regroup(63)
        row_copies = send_halo_rows(first)

        def inner(x):
            regroup(x + 1)

        loop(62, inner)
        copies = widen(first, row_copies)
        g.cot[...] = cot_ref[...].astype(f32)
        fill_wide(first, copies)
        convolve(first, 0)
        loads[1].wait()
        loads[2].wait()

    to_modes(first, lambda i: v_ref.at[i], cover_field, nothing)
    loads[3].wait()
    for kl in range(4):

        def add_channel(i, sums):
            real, imag = sums
            s_re = first.modes[pl.ds(8 * i + kl, 1), :][:, :32]
            s_im = first.modes[pl.ds(8 * i + 4 + kl, 1), :][:, :32]
            w_re = g.weight[kl, 0, i].astype(f32)
            w_im = g.weight[kl, 1, i].astype(f32)
            return (real + (w_re * s_re - w_im * s_im), imag + (w_re * s_im + w_im * s_re))

        zero = jnp.zeros((32, 32), f32)
        real, imag = lax.fori_loop(0, 32, add_channel, (zero, zero))
        factor = jnp.where(row_at * 4 + kl == 0, 1.0, 2.0).astype(f32) * scale
        g.mix[32 * kl : 32 * kl + 32, 0:32] = real.astype(bf16).astype(f32) * factor
        g.mix[128 + 32 * kl : 160 + 32 * kl, 0:32] = imag.astype(bf16).astype(f32) * factor
    to_grid(first, nothing)

    bias = jnp.broadcast_to(bias_ref[...], (32, 256))
    proj = jnp.broadcast_to(proj_ref[...], (32, 256))

    def activate(x, sums):
        bias_sum, proj_sum = sums
        pre = g.cells[pl.ds(aligned(x * 32, 32), 32), :] + grid_row(x) + bias
        cdf = 0.5 * (1.0 + lax.erf(pre * math.sqrt(0.5)))
        pdf = jnp.exp(-0.5 * pre * pre) * (1.0 / math.sqrt(TWO_PI))
        cot = jnp.broadcast_to(g.cot[pl.ds(x, 1), :], (32, 256))
        grad = (proj * cot) * (cdf + pre * pdf)
        rounded = grad.astype(bf16)
        second.raw[pl.ds(aligned(x * 32 + 32, 32), 32), :] = rounded
        put_grid_row(x, rounded.astype(f32))
        return (bias_sum + grad, proj_sum + (pre * cdf) * cot)

    zero = jnp.zeros((32, 256), f32)
    bias_sum, proj_sum = lax.fori_loop(0, 64, activate, (zero, zero))
    for i in range(n_col):
        second.snd1[i] = placed(i).astype(bf16)

    piece = 80 // owners

    def cover_grad():
        row_copies = send_halo_rows(second)
        g.sums[0:32] = bias_sum
        g.sums[32:64] = proj_sum
        g.sums[64:128] = jnp.zeros((64, 256), f32)
        g.outer[...] = jnp.zeros_like(g.outer)

        def block(t):
            rows = first.wide[pl.ds(aligned(t * 768, 16), 960), :]
            grads = second.raw[pl.ds(aligned(t * 256 + 32, 32), 256), :]
            g.outer[...] += dot(rows, grads, NT)

        loop(8, block)
        copies = widen(second, row_copies)
        lane = lax.broadcasted_iota(jnp.int32, (96, 128), 1)
        taps = []
        for a in range(3):
            total = jnp.zeros((96, 128), f32)
            for x in range(8):
                here = g.outer[96 * (x + a) : 96 * (x + a) + 96, 128 * (x // 4) : 128 * (x // 4) + 128]
                total = total + (pltpu.roll(here, 128 - 32 * (x % 4), 1) if x % 4 else here)
            taps.append(jnp.where(lane < 32, total, 0.0))
        taps = jnp.concatenate(taps, axis=0)
        packed = taps[0:72]
        for q in range(1, 4):
            packed = packed + pltpu.roll(taps[72 * q : 72 * q + 72], 32 * q, 1)
        lanes_sum = lax.dot_general(
            jnp.ones((8, 256), f32), g.sums[...], NT, precision=HIGH, preferred_element_type=f32
        )
        g.part[...] = (jnp.concatenate([packed, lanes_sum], axis=0) * scale).reshape(owners, piece, 128)
        for t in range(owners):

            @pl.when(row_at != t)
            def _():
                push(g.part.at[t], g.got_row.at[row_at], g.row_s.at[t], g.row_r.at[row_at], "row", t).start()

        fill_wide(second, copies)
        convolve(second, 1)

    def sum_rows():
        @pl.when(row_at < owners)
        def _():
            g.got_row[row_at] = g.part[row_at]

            def wait(d):
                origin = lax.rem(row_at + d, n_row)
                push(g.part.at[0], g.got_row.at[origin], g.row_s.at[0], g.row_r.at[origin], "row", origin).wait_recv()

            each(n_row, wait)
            g.sum_row[...] = jnp.sum(g.got_row[...], axis=0)
            g.got_col[col_at] = g.sum_row[...]
            start, _, _ = exchange(
                "col", col_at, n_col, lambda i: g.sum_row, lambda i: g.got_col.at[i], g.col_s, g.col_r
            )
            each(n_col, start)

    def sum_cols():
        @pl.when(row_at < owners)
        def _():
            _, sent, got = exchange(
                "col", col_at, n_col, lambda i: g.sum_row, lambda i: g.got_col.at[i], g.col_s, g.col_r
            )
            each(n_col, got)
            each(n_col, sent)
            g.total[...] = jnp.sum(g.got_col[...], axis=0)
            g.got_all[row_at] = g.total[...]

            def send(d):
                peer = lax.rem(row_at + d, n_row)
                push(g.total, g.got_all.at[row_at], g.all_s.at[d], g.all_r.at[row_at], "row", peer).start()

            each(n_row, send)

    to_modes(second, lambda i: second.snd1.at[i], cover_grad, sum_rows)
    for kl in range(4):
        factor = jnp.where(row_at * 4 + kl == 0, 1.0, 2.0).astype(f32)
        g_re = second.modes[pl.ds(kl, 32, stride=8), :][:, :32] * factor
        g_im = second.modes[pl.ds(4 + kl, 32, stride=8), :][:, :32] * factor

        def one_channel(i, carry):
            s_re = first.modes[pl.ds(8 * i + kl, 1), :][:, :32]
            s_im = first.modes[pl.ds(8 * i + 4 + kl, 1), :][:, :32]
            w_re = g.weight[kl, 0, i].astype(f32)
            w_im = g.weight[kl, 1, i].astype(f32)
            gspec_ref[kl, 0, i] = g_re * s_re + g_im * s_im
            gspec_ref[kl, 1, i] = g_im * s_re - g_re * s_im
            b_re = jnp.sum(w_re * g_re + w_im * g_im, axis=0, keepdims=True)
            b_im = jnp.sum(w_re * g_im - w_im * g_re, axis=0, keepdims=True)
            g.mix[pl.ds(32 * kl + i, 1), 0:32] = b_re.astype(bf16).astype(f32) * scale
            g.mix[pl.ds(128 + 32 * kl + i, 1), 0:32] = b_im.astype(bf16).astype(f32) * scale
            return carry

        lax.fori_loop(0, 32, one_channel, 0)
    to_grid(second, sum_cols)

    def finish(x):
        put_grid_row(x, g.cells[pl.ds(aligned(x * 32, 32), 32), :] + grid_row(x))

    loop(64, finish)
    for i in range(n_col):
        out_ref[256 * i : 256 * i + 256] = placed(i)
    for t in range(owners):

        @pl.when(row_at != t)
        def _():
            arrived = push(g.part.at[t], g.got_all.at[t], g.row_s.at[t], g.all_r.at[t], "row", t)
            arrived.wait_recv()
            arrived.wait_send()

    @pl.when(row_at < owners)
    def _():
        def sent(d):
            peer = lax.rem(row_at + d, n_row)
            push(g.total, g.got_all.at[row_at], g.all_s.at[d], g.all_r.at[row_at], "row", peer).wait_send()

        each(n_row, sent)

    small_ref[...] = g.got_all[...].reshape(80, 128)
    for wait in pending:
        wait()


def per_device(n_row, n_col, ocean_field, cotangent, conv_weight, conv_bias, projection, mode_weight):
    chans, rows_dev, cols_dev = ocean_field.shape
    ky_dev = mode_weight.shape[0]
    kx_all = mode_weight.shape[4] * n_col
    owners = min(10, n_row)
    ty, tx = (jnp.asarray(t) for t in tables(n_row, n_col, ky_dev, rows_dev, cols_dev, kx_all))
    taps = conv_weight.astype(jnp.float32)
    straight = jnp.transpose(taps, (3, 0, 1, 2)).reshape(chans, 9 * chans)
    turned = jnp.transpose(taps[::-1, ::-1], (2, 0, 1, 3)).reshape(chans, 9 * chans)
    both = jnp.pad(jnp.stack([straight, turned]), ((0, 0), (0, 0), (0, 1024 - 9 * chans)))
    vmem = pl.BlockSpec(memory_space=pltpu.VMEM)
    hbm = pl.BlockSpec(memory_space=pl.ANY)
    one = pass_scratch(n_row, n_col)
    scratch = list(one.values()) * 2 + list(common_scratch(n_row, n_col, rows_dev * n_row, owners).values())
    cells, grad_spec, small = pl.pallas_call(
        functools.partial(step_kernel, n_row, n_col, owners),
        out_shape=[
            jax.ShapeDtypeStruct((chans * rows_dev, cols_dev), jnp.float32),
            jax.ShapeDtypeStruct(mode_weight.shape, jnp.float32),
            jax.ShapeDtypeStruct((80, 128), jnp.float32),
        ],
        in_specs=[hbm, vmem, vmem, vmem, vmem, hbm, hbm, hbm],
        out_specs=[vmem, vmem, vmem],
        scratch_shapes=scratch,
        compiler_params=pltpu.CompilerParams(
            collective_id=0, has_side_effects=True, vmem_limit_bytes=VMEM_BYTES
        ),
        name="layer_step",
    )(
        ocean_field.reshape(n_col, 256, cols_dev),
        cotangent,
        both,
        conv_bias.reshape(chans, 1),
        projection.reshape(chans, 1),
        mode_weight,
        ty,
        tx,
    )
    grad_conv = jnp.transpose(small[:72].reshape(72, 4, 32), (1, 0, 2)).reshape(conv_weight.shape)
    return (cells.reshape(ocean_field.shape), grad_spec, grad_conv, small[72, :32], small[72, 32:64])


def solution(mesh):
    placed = (
        P(None, "row", "col"),
        P("row", "col"),
        P(),
        P(),
        P(),
        P("row", None, None, None, "col"),
    )
    return jax.shard_map(
        functools.partial(per_device, mesh.shape["row"], mesh.shape["col"]),
        mesh=mesh,
        in_specs=placed,
        out_specs=(P(None, "row", "col"), P("row", None, None, None, "col"), P(), P(), P()),
        check_vma=False,
    )
```

time: 318 us -> 179 us (0.56)
  blocking collectives: 80.3 us -> 0 us
  matrix products: 37.2 us -> 0 us
  Pallas kernels: 140 us -> 165 us
  starting transfers between devices: 22 us -> 0 us
  local copies, waits for them, and re-layouts: 26.3 us -> 11.3 us
  other arithmetic: 10.1 us -> 1.64 us
    psum x1 -> x0, blocking collectives: 80.3 us -> none  [per_device(): lax.psum((kernel_part, bias_part, proj_part), ('row', 'col'))]
    dot_general x27 -> x0, matrix products: 37.2 us -> none  [the longest x9 22.1 us: conv_cells(): jnp.einsum('io,ixy->oxy', kernel[tap_row, tap_col], shifted, preferred_el...]
    pallas_call x2 -> x1, Pallas kernels: 140 us -> 165 us  [per_device(): pl.pallas_call(functools.partial(step_kernel, n_row, n_col, owners), out_...]
    ppermute x8 -> x0, starting transfers between devices: 22 us -> none  [the longest x4 11 us: with_halo(): after = lax.ppermute(first, axis, down)]
    slice x8 -> x2, local copies, waits for them, and re-layouts: 7.83 us -> 0.86 us  [per_device(): small[:72].reshape(72, 4, 32)]
    convert_element_type x4 -> x1, other arithmetic: 6.43 us -> 0.9 us  [per_device(): taps = conv_weight.astype(jnp.float32)]
    ppermute x4 -> x0, local copies, waits for them, and re-layouts: 5.34 us -> none  [the longest x2 2.71 us: with_halo(): before = lax.ppermute(last, axis, up)]
    unnamed x47 -> x5, local copies, waits for them, and re-layouts: 10.9 us -> 6.07 us
  transfers between devices with their start and end apart: 8 -> 0, of which waited for: 0 -> 0; matrix products, arithmetic and copies ran while one was open for 11% -> 0% of each run, Pallas kernels for 44% -> 0%
where the time goes in v2:
time: 179 us
  Pallas kernels  165 us (92%)
  local copies, waits for them, and re-layouts  11.3 us (6%)
    pallas_call x1, Pallas kernels, per_device(): pl.pallas_call(functools.partial(step_kernel, n_row, n_col, owners), out_...  165 us
    unnamed x5, local copies, waits for them, and re-layouts  6.07 us

profile of v2, /device:TPU:1, one launch (start us, length us, event | category | flops | bytes accessed | tf_op | source)
XLA Modules:
  0.0 178.7 jit_solution(9515107288486615277)
XLA Ops:
  0.6 0.9 convert_element_type.5
  1.5 0.1 copy.24
  1.7 0.1 stack_reshape.7
  1.8 0.1 copy.30
  1.9 0.7 select_maximum_fusion.refs_2_
  2.6 1.3 copy.25.refs_3_
  4.0 1.3 copy.26.refs_4_
  5.3 165.2 %layer_step.1 = (f32[2048,256]{1,0:T(8,128)}, f32[4,2,32,32,32]{4,3,2,1,0:T(8,128)}, f32[80,128]{1,0:T(8,128)}) custom-call(bf16[8,256,256]{2,1,0:T(8,128)(2,1)} %bitcast.19, bf16[64,256]{1,0:T(8,128)(2,1)} %refs_1_.1, f32[2,32,1024]{2,1,0:T(8,128)} %select_maximum_fusion.refs_2_, f32[32,1]{1,0:T(8,128)} %copy.25.refs_3_, f32[32,1]{1,0:T(8,128)} %copy.26.refs_4_, ...), custom_call_target="tpu_custom_call" | custom-call | tf_op jit(solution)/shard_map/layer_step/pallas_call | solution.py:607
  170.5 0.8 slice.9
  171.3 0.1 copy.27
  171.3 0.8 copy.31
  172.1 1.3 slice_bitcast_fusion
  173.5 0.0 copy-start
  173.5 3.3 %copy.35 = f32[32,64,256]{2,1,0:T(8,128)} copy(f32[32,64,256]{2,1,0:T(8,128)} %bitcast.17) | data formatting | bytes 4194304
  176.7 0.0 copy-done
  176.7 2.0 %copy.36 = f32[4,2,32,32,32]{4,3,2,1,0:T(8,128)} copy(f32[4,2,32,32,32]{4,3,2,1,0:T(8,128)S(1)} %copy-done) | data formatting | bytes 2097152
  (1 shorter events, 0.0 us)
Async XLA Ops:
  173.5 3.3 %copy-start = (f32[4,2,32,32,32]{4,3,2,1,0:T(8,128)S(1)}, f32[4,2,32,32,32]{4,3,2,1,0:T(8,128)}, u32[]{:S(2)}) copy-start(f32[4,2,32,32,32]{4,3,2,1,0:T(8,128)} %get-tuple-element.24) | copy-start | bytes 3145732

commit v3 on v2

--- a/solution.py
+++ b/solution.py
@@ -12,6 +12,7 @@
 
 TWO_PI = 2.0 * math.pi
 HIGH = lax.Precision.HIGHEST
+HALF_FILL = 8
 VMEM_BYTES = 56 * 1024 * 1024
 
 
@@ -171,7 +172,7 @@
 
 
 def step_kernel(n_row, n_col, owners, *refs):
-    (v_ref, cot_ref, w2_ref, bias_ref, proj_ref, w_hbm, ty_hbm, tx_hbm, out_ref, gspec_ref, small_ref, *rest) = refs
+    (v_ref, cot_ref, taps_ref, bias_ref, proj_ref, w_hbm, ty_hbm, tx_hbm, out_ref, modes_ref, small_ref, *rest) = refs
     nx = 64 * n_row
     names = list(pass_scratch(n_row, n_col))
     first = Group(names, rest[: len(names)])
@@ -243,9 +244,7 @@
             pending.append(copy.wait_send)
         return copies
 
-    def fill_wide(p, copies):
-        for copy in copies:
-            copy.wait_recv()
+    def fill_wide(p, start, stop):
         row = lax.broadcasted_iota(jnp.int32, (16, 128), 0)
         lane = lax.broadcasted_iota(jnp.int32, (16, 128), 1)
         put_left = jnp.where((row == 0) & (lane == 0) & (col_at > 0), 1.0, 0.0).astype(bf16)
@@ -265,13 +264,20 @@
                     base = aligned(q * 384 + 96 * x + 32 * b, 32)
                     p.wide[pl.ds(base, 32), :] = value[32 * x : 32 * x + 32].astype(bf16)
 
-        loop(17, chunk)
-
-    def convolve(p, kernel):
-        padded = w2_ref[kernel]
+        loop(stop - start, lambda q: chunk(q + start))
+
+    def spread_taps(p, turned):
+        row = lax.broadcasted_iota(jnp.int32, (32, 1024), 0)
+        lane = lax.broadcasted_iota(jnp.int32, (32, 1024), 1)
+        padded = jnp.zeros((32, 1024), f32)
+        for m in range(9):
+            source = 8 - m if turned else m
+            spot = jnp.where(lane == row + 32 * m, 1.0, 0.0).astype(bf16)
+            padded = padded + dot(taps_ref[32 * source : 32 * source + 32, :], spot, NN if turned else TN)
         for x in range(8):
             p.taps[32 * x : 32 * x + 32, :] = (pltpu.roll(padded, 96 * x, 1) if x else padded).astype(bf16)
 
+    def convolve(p):
         def block(t):
             rows = p.wide[pl.ds(aligned(t * 768, 16), 1024), :]
             g.cells[pl.ds(aligned(t * 256, 256), 256), :] = dot(p.taps[...], rows, NN)
@@ -326,7 +332,7 @@
         for i in range(n_col):
             p.modes[32 * i : 32 * i + 32] = pltpu.roll(p.rcv5[i].astype(f32), back_shift, 1)
 
-    def to_grid(p, cover_rows):
+    def to_grid(p, cover_rows, cover_cells):
         g.mix[...] = pltpu.roll(g.mix[...], quarter, 1)
         for i in range(n_col):
             for odd_channel in range(2):
@@ -372,7 +378,7 @@
 
         each(n_col, make_cells)
         pending.append(lambda: each(n_col, sent10))
-
+        cover_cells()
         place(col_at, dot(lhs, g.ty[col_at], NN))
 
         def take(d):
@@ -383,6 +389,10 @@
 
     def nothing():
         return None
+
+    def rest_of_conv(p):
+        fill_wide(p, HALF_FILL, 17)
+        convolve(p)
 
     def place(slot, value):
         for half in range(2):
@@ -422,8 +432,10 @@
         loop(62, inner)
         copies = widen(first, row_copies)
         g.cot[...] = cot_ref[...].astype(f32)
-        fill_wide(first, copies)
-        convolve(first, 0)
+        spread_taps(first, False)
+        for copy in copies:
+            copy.wait_recv()
+        fill_wide(first, 0, HALF_FILL)
         loads[1].wait()
         loads[2].wait()
 
@@ -444,10 +456,15 @@
         factor = jnp.where(row_at * 4 + kl == 0, 1.0, 2.0).astype(f32) * scale
         g.mix[32 * kl : 32 * kl + 32, 0:32] = real.astype(bf16).astype(f32) * factor
         g.mix[128 + 32 * kl : 160 + 32 * kl, 0:32] = imag.astype(bf16).astype(f32) * factor
-    to_grid(first, nothing)
-
-    bias = jnp.broadcast_to(bias_ref[...], (32, 256))
-    proj = jnp.broadcast_to(proj_ref[...], (32, 256))
+    to_grid(first, nothing, lambda: rest_of_conv(first))
+
+    def column(ref):
+        diagonal = lax.broadcasted_iota(jnp.int32, (32, 32), 0) == lax.broadcasted_iota(jnp.int32, (32, 32), 1)
+        value = jnp.sum(jnp.where(diagonal, jnp.broadcast_to(ref[...], (32, 32)), 0.0), axis=1, keepdims=True)
+        return jnp.broadcast_to(value, (32, 256))
+
+    bias = column(bias_ref)
+    proj = column(proj_ref)
 
     def activate(x, sums):
         bias_sum, proj_sum = sums
@@ -504,8 +521,10 @@
             def _():
                 push(g.part.at[t], g.got_row.at[row_at], g.row_s.at[t], g.row_r.at[row_at], "row", t).start()
 
-        fill_wide(second, copies)
-        convolve(second, 1)
+        spread_taps(second, True)
+        for copy in copies:
+            copy.wait_recv()
+        fill_wide(second, 0, HALF_FILL)
 
     def sum_rows():
         @pl.when(row_at < owners)
@@ -542,18 +561,15 @@
             each(n_row, send)
 
     to_modes(second, lambda i: second.snd1.at[i], cover_grad, sum_rows)
+    own_mode = lax.broadcasted_iota(jnp.int32, (256, 128), 0) & 3
+    second.modes[...] = second.modes[...] * jnp.where(row_at * 4 + own_mode == 0, 1.0, 2.0)
     for kl in range(4):
-        factor = jnp.where(row_at * 4 + kl == 0, 1.0, 2.0).astype(f32)
-        g_re = second.modes[pl.ds(kl, 32, stride=8), :][:, :32] * factor
-        g_im = second.modes[pl.ds(4 + kl, 32, stride=8), :][:, :32] * factor
+        g_re = second.modes[pl.ds(kl, 32, stride=8), :][:, :32]
+        g_im = second.modes[pl.ds(4 + kl, 32, stride=8), :][:, :32]
 
         def one_channel(i, carry):
-            s_re = first.modes[pl.ds(8 * i + kl, 1), :][:, :32]
-            s_im = first.modes[pl.ds(8 * i + 4 + kl, 1), :][:, :32]
             w_re = g.weight[kl, 0, i].astype(f32)
             w_im = g.weight[kl, 1, i].astype(f32)
-            gspec_ref[kl, 0, i] = g_re * s_re + g_im * s_im
-            gspec_ref[kl, 1, i] = g_im * s_re - g_re * s_im
             b_re = jnp.sum(w_re * g_re + w_im * g_im, axis=0, keepdims=True)
             b_im = jnp.sum(w_re * g_im - w_im * g_re, axis=0, keepdims=True)
             g.mix[pl.ds(32 * kl + i, 1), 0:32] = b_re.astype(bf16).astype(f32) * scale
@@ -561,11 +577,13 @@
             return carry
 
         lax.fori_loop(0, 32, one_channel, 0)
-    to_grid(second, sum_cols)
+    to_grid(second, sum_cols, lambda: rest_of_conv(second))
 
     def finish(x):
         put_grid_row(x, g.cells[pl.ds(aligned(x * 32, 32), 32), :] + grid_row(x))
 
+    modes_ref[0] = first.modes[...]
+    modes_ref[1] = second.modes[...]
     loop(64, finish)
     for i in range(n_col):
         out_ref[256 * i : 256 * i + 256] = placed(i)
@@ -588,6 +606,28 @@
     small_ref[...] = g.got_all[...].reshape(80, 128)
     for wait in pending:
         wait()
+
+
+def outputs_kernel(cells_ref, modes_ref, small_ref, out_ref, gspec_ref, conv_ref, bias_ref, proj_ref):
+    out_ref[...] = cells_ref[...]
+    kl = pl.program_id(0) // 2
+    first = lax.rem(pl.program_id(0), 2) * 16
+    g_re = modes_ref[pl.ds(256 + kl, 32, stride=8), :][:, :32]
+    g_im = modes_ref[pl.ds(260 + kl, 32, stride=8), :][:, :32]
+    for i in range(16):
+        s_re = modes_ref[pl.ds(8 * (first + i) + kl, 1), :][:, :32]
+        s_im = modes_ref[pl.ds(8 * (first + i) + 4 + kl, 1), :][:, :32]
+        gspec_ref[0, 0, i] = g_re * s_re + g_im * s_im
+        gspec_ref[0, 1, i] = g_im * s_re - g_re * s_im
+
+    @pl.when(pl.program_id(0) == 0)
+    def _():
+        for q in range(4):
+            rows = small_ref[0:72]
+            conv_ref[72 * q : 72 * q + 72] = (pltpu.roll(rows, 128 - 32 * q, 1) if q else rows)[:, :32]
+        rows = small_ref[72:80]
+        bias_ref[...] = rows[0:1, :32]
+        proj_ref[...] = pltpu.roll(rows, 96, 1)[0:1, :32]
 
 
 def per_device(n_row, n_col, ocean_field, cotangent, conv_weight, conv_bias, projection, mode_weight):
@@ -596,19 +636,15 @@
     kx_all = mode_weight.shape[4] * n_col
     owners = min(10, n_row)
     ty, tx = (jnp.asarray(t) for t in tables(n_row, n_col, ky_dev, rows_dev, cols_dev, kx_all))
-    taps = conv_weight.astype(jnp.float32)
-    straight = jnp.transpose(taps, (3, 0, 1, 2)).reshape(chans, 9 * chans)
-    turned = jnp.transpose(taps[::-1, ::-1], (2, 0, 1, 3)).reshape(chans, 9 * chans)
-    both = jnp.pad(jnp.stack([straight, turned]), ((0, 0), (0, 0), (0, 1024 - 9 * chans)))
     vmem = pl.BlockSpec(memory_space=pltpu.VMEM)
     hbm = pl.BlockSpec(memory_space=pl.ANY)
     one = pass_scratch(n_row, n_col)
     scratch = list(one.values()) * 2 + list(common_scratch(n_row, n_col, rows_dev * n_row, owners).values())
-    cells, grad_spec, small = pl.pallas_call(
+    cells, modes, small = pl.pallas_call(
         functools.partial(step_kernel, n_row, n_col, owners),
         out_shape=[
             jax.ShapeDtypeStruct((chans * rows_dev, cols_dev), jnp.float32),
-            jax.ShapeDtypeStruct(mode_weight.shape, jnp.float32),
+            jax.ShapeDtypeStruct((2, 256, 128), jnp.float32),
             jax.ShapeDtypeStruct((80, 128), jnp.float32),
         ],
         in_specs=[hbm, vmem, vmem, vmem, vmem, hbm, hbm, hbm],
@@ -621,15 +657,42 @@
     )(
         ocean_field.reshape(n_col, 256, cols_dev),
         cotangent,
-        both,
-        conv_bias.reshape(chans, 1),
-        projection.reshape(chans, 1),
+        conv_weight.reshape(9 * chans, chans),
+        conv_bias.reshape(1, chans),
+        projection.reshape(1, chans),
         mode_weight,
         ty,
         tx,
     )
-    grad_conv = jnp.transpose(small[:72].reshape(72, 4, 32), (1, 0, 2)).reshape(conv_weight.shape)
-    return (cells.reshape(ocean_field.shape), grad_spec, grad_conv, small[72, :32], small[72, 32:64])
+    whole = lambda *shape: pl.BlockSpec(shape, lambda t: (0,) * len(shape))
+    grad_input, grad_spec, grad_conv, grad_bias, grad_proj = pl.pallas_call(
+        outputs_kernel,
+        grid=(8,),
+        out_shape=[
+            jax.ShapeDtypeStruct((chans * rows_dev, cols_dev), jnp.float32),
+            jax.ShapeDtypeStruct(mode_weight.shape, jnp.float32),
+            jax.ShapeDtypeStruct((9 * chans, chans), jnp.float32),
+            jax.ShapeDtypeStruct((1, chans), jnp.float32),
+            jax.ShapeDtypeStruct((1, chans), jnp.float32),
+        ],
+        in_specs=[pl.BlockSpec((256, 256), lambda t: (t, 0)), whole(512, 128), whole(80, 128)],
+        out_specs=[
+            pl.BlockSpec((256, 256), lambda t: (t, 0)),
+            pl.BlockSpec((1, 2, 16, 32, 32), lambda t: (t // 2, 0, t % 2, 0, 0)),
+            whole(9 * chans, chans),
+            whole(1, chans),
+            whole(1, chans),
+        ],
+        compiler_params=pltpu.CompilerParams(vmem_limit_bytes=VMEM_BYTES),
+        name="layer_outputs",
+    )(cells, modes.reshape(512, 128), small)
+    return (
+        grad_input.reshape(ocean_field.shape),
+        grad_spec,
+        grad_conv.reshape(conv_weight.shape),
+        grad_bias.reshape(chans),
+        grad_proj.reshape(chans),
+    )
 
 
 def solution(mesh):

time: 179 us -> 163 us (0.911)
  local copies, waits for them, and re-layouts: 11.3 us -> 0 us
  Pallas kernels: 165 us -> 162 us
    pallas_call x1, Pallas kernels: 165 us -> 155 us  [per_device(): pl.pallas_call(functools.partial(step_kernel, n_row, n_col, owners), out_...]
    pallas_call x0 -> x1, Pallas kernels: none -> 6.75 us  [per_device(): pl.pallas_call(outputs_kernel, grid=(8,), out_shape=[jax.ShapeDtypeStruct...]
    unnamed x5 -> x0, local copies, waits for them, and re-layouts: 6.07 us -> none
    reshape x2 -> x0, local copies, waits for them, and re-layouts: 2.68 us -> none  [the longest x1 1.34 us: per_device(): conv_bias.reshape(chans, 1)]
where the time goes in v3:
time: 163 us
  Pallas kernels  162 us (99%)
    pallas_call x1, Pallas kernels, per_device(): pl.pallas_call(functools.partial(step_kernel, n_row, n_col, owners), out_...  155 us
    pallas_call x1, Pallas kernels, per_device(): pl.pallas_call(outputs_kernel, grid=(8,), out_shape=[jax.ShapeDtypeStruct...  6.75 us

profile of v3, /device:TPU:1, one launch (start us, length us, event | category | flops | bytes accessed | tf_op | source)
XLA Modules:
  0.0 162.9 jit_solution(635525637122465607)
XLA Ops:
  0.6 155.5 %layer_step.1 = (f32[2048,256]{1,0:T(8,128)}, f32[2,256,128]{2,1,0:T(8,128)}, f32[80,128]{1,0:T(8,128)}) custom-call(bf16[8,256,256]{2,1,0:T(8,128)(2,1)} %bitcast.9, bf16[64,256]{1,0:T(8,128)(2,1)} %refs_1_.1, bf16[288,32]{1,0:T(8,128)(2,1)} %bitcast.11, f32[1,32]{1,0:T(1,128)} %bitcast.12, f32[1,32]{1,0:T(1,128)} %bitcast.13, ...), custom_call_target="tpu_custom_call" | custom-call | tf_op jit(solution)/shard_map/layer_step/pallas_call | solution.py:643
  156.1 6.8 %layer_outputs.1 = (f32[2048,256]{1,0:T(8,128)}, f32[4,2,32,32,32]{4,3,2,1,0:T(8,128)}, f32[288,32]{1,0:T(8,128)}, f32[1,32]{1,0:T(1,128)}, f32[1,32]{1,0:T(1,128)}) custom-call(f32[2048,256]{1,0:T(8,128)} %get-tuple-element.13.cells_ref, f32[512,128]{1,0:T(8,128)} %bitcast.10, f32[80,128]{1,0:T(8,128)} %get-tuple-element.15.small_ref), custom_call_target="tpu_custom_call" | custom-call | tf_op jit(solution)/shard_map/layer_outputs/pallas_call | solution.py:668

commit v4 on v3

--- a/solution.py
+++ b/solution.py
@@ -148,7 +148,10 @@
         tx=pltpu.VMEM((512, nx), bf16),
         weight=pltpu.VMEM((4, 2, 32, 32, 32), bf16),
         stage=pltpu.VMEM((4096, 128), f32),
-        cells=pltpu.VMEM((2048, 256), f32),
+        bias=pltpu.VMEM((32, 256), f32),
+        proj=pltpu.VMEM((32, 256), f32),
+        bias_rows=pltpu.VMEM((256, 256), f32),
+        proj_rows=pltpu.VMEM((256, 256), f32),
         cot=pltpu.VMEM((64, 256), f32),
         acc=pltpu.VMEM((8 * n_row, 256), f32),
         rows_x=pltpu.VMEM((32, nx), bf16),
@@ -280,15 +283,18 @@
     def convolve(p):
         def block(t):
             rows = p.wide[pl.ds(aligned(t * 768, 16), 1024), :]
-            g.cells[pl.ds(aligned(t * 256, 256), 256), :] = dot(p.taps[...], rows, NN)
+            result = dot(p.taps[...], rows, NN)
+            for x in range(8):
+                put_grid_row(8 * t + x, result[32 * x : 32 * x + 32])
 
         loop(8, block)
 
-    def to_modes(p, source, cover, cover_rows):
+    def to_modes(p, source, started, cover, cover_rows):
         own = pltpu.make_async_copy(source(col_at), p.buf1.at[col_at], p.own)
         own.start()
         start, sent, got = exchange("col", col_at, n_col, source, lambda i: p.buf1.at[i], p.s1, p.r1)
-        each(n_col, start)
+        if not started:
+            each(n_col, start)
         pending.append(lambda: each(n_col, sent))
         cover()
         own.wait()
@@ -332,7 +338,7 @@
         for i in range(n_col):
             p.modes[32 * i : 32 * i + 32] = pltpu.roll(p.rcv5[i].astype(f32), back_shift, 1)
 
-    def to_grid(p, cover_rows, cover_cells):
+    def to_grid(p, cover_rows, cover_cells, use):
         g.mix[...] = pltpu.roll(g.mix[...], quarter, 1)
         for i in range(n_col):
             for odd_channel in range(2):
@@ -379,28 +385,42 @@
         each(n_col, make_cells)
         pending.append(lambda: each(n_col, sent10))
         cover_cells()
-        place(col_at, dot(lhs, g.ty[col_at], NN))
+        use(col_at, dot(lhs, g.ty[col_at], NN), 0)
 
         def take(d):
             origin = got10(d)
-            place(origin, p.rcv10[origin].astype(f32))
+            use(origin, p.rcv10[origin].astype(f32), d)
 
         each(n_col, take)
 
-    def nothing():
-        return None
+    def first_fill(p):
+        for copy in p.edge_copies:
+            copy.wait_recv()
+        fill_wide(p, 0, HALF_FILL)
 
     def rest_of_conv(p):
         fill_wide(p, HALF_FILL, 17)
         convolve(p)
 
+    def regroup(p):
+        def one(x):
+            p.raw[pl.ds(aligned(x * 32 + 32, 32), 32), :] = grid_row(x).astype(bf16)
+
+        one(0)
+        one(63)
+        p.row_copies = send_halo_rows(p)
+        loop(62, lambda x: one(x + 1))
+
+    def widen_now(p):
+        p.edge_copies = widen(p, p.row_copies)
+
     def place(slot, value):
         for half in range(2):
             g.stage[pl.ds(aligned(half * 2048 + slot * 256, 256), 256), :] = value[:, 128 * half : 128 * half + 128]
 
     def placed(slot):
         return jnp.concatenate(
-            [g.stage[2048 * half + 256 * slot : 2048 * half + 256 * slot + 256] for half in range(2)], axis=1
+            [g.stage[pl.ds(aligned(half * 2048 + slot * 256, 256), 256), :] for half in range(2)], axis=1
         )
 
     def grid_row(x):
@@ -419,27 +439,20 @@
         for i in range(n_col):
             place(i, g.vbuf[i].astype(f32))
 
-        def regroup(x):
-            first.raw[pl.ds(aligned(x * 32 + 32, 32), 32), :] = grid_row(x).astype(bf16)
-
-        regroup(0)
-        regroup(63)
-        row_copies = send_halo_rows(first)
-
-        def inner(x):
-            regroup(x + 1)
-
-        loop(62, inner)
-        copies = widen(first, row_copies)
+        regroup(first)
         g.cot[...] = cot_ref[...].astype(f32)
         spread_taps(first, False)
-        for copy in copies:
-            copy.wait_recv()
-        fill_wide(first, 0, HALF_FILL)
+        g.bias[...] = column(bias_ref)
+        g.proj[...] = column(proj_ref)
         loads[1].wait()
         loads[2].wait()
 
-    to_modes(first, lambda i: v_ref.at[i], cover_field, nothing)
+    def column(ref):
+        diagonal = lax.broadcasted_iota(jnp.int32, (32, 32), 0) == lax.broadcasted_iota(jnp.int32, (32, 32), 1)
+        value = jnp.sum(jnp.where(diagonal, jnp.broadcast_to(ref[...], (32, 32)), 0.0), axis=1, keepdims=True)
+        return jnp.broadcast_to(value, (32, 256))
+
+    to_modes(first, lambda i: v_ref.at[i], False, cover_field, lambda: widen_now(first))
     loads[3].wait()
     for kl in range(4):
 
@@ -456,39 +469,46 @@
         factor = jnp.where(row_at * 4 + kl == 0, 1.0, 2.0).astype(f32) * scale
         g.mix[32 * kl : 32 * kl + 32, 0:32] = real.astype(bf16).astype(f32) * factor
         g.mix[128 + 32 * kl : 160 + 32 * kl, 0:32] = imag.astype(bf16).astype(f32) * factor
-    to_grid(first, nothing, lambda: rest_of_conv(first))
-
-    def column(ref):
-        diagonal = lax.broadcasted_iota(jnp.int32, (32, 32), 0) == lax.broadcasted_iota(jnp.int32, (32, 32), 1)
-        value = jnp.sum(jnp.where(diagonal, jnp.broadcast_to(ref[...], (32, 32)), 0.0), axis=1, keepdims=True)
-        return jnp.broadcast_to(value, (32, 256))
-
-    bias = column(bias_ref)
-    proj = column(proj_ref)
-
-    def activate(x, sums):
-        bias_sum, proj_sum = sums
-        pre = g.cells[pl.ds(aligned(x * 32, 32), 32), :] + grid_row(x) + bias
-        cdf = 0.5 * (1.0 + lax.erf(pre * math.sqrt(0.5)))
-        pdf = jnp.exp(-0.5 * pre * pre) * (1.0 / math.sqrt(TWO_PI))
-        cot = jnp.broadcast_to(g.cot[pl.ds(x, 1), :], (32, 256))
-        grad = (proj * cot) * (cdf + pre * pdf)
-        rounded = grad.astype(bf16)
-        second.raw[pl.ds(aligned(x * 32 + 32, 32), 32), :] = rounded
-        put_grid_row(x, rounded.astype(f32))
-        return (bias_sum + grad, proj_sum + (pre * cdf) * cot)
-
-    zero = jnp.zeros((32, 256), f32)
-    bias_sum, proj_sum = lax.fori_loop(0, 64, activate, (zero, zero))
-    for i in range(n_col):
-        second.snd1[i] = placed(i).astype(bf16)
+
+    back_start, _, _ = exchange(
+        "col", col_at, n_col, lambda i: second.snd1.at[i], lambda i: second.buf1.at[i], second.s1, second.r1
+    )
+
+    def activate(slot, cells, d):
+        conv = placed(slot)
+        rounded = []
+        for ch in range(4):
+            channel = slot * 4 + ch
+            rows = slice(64 * ch, 64 * ch + 64)
+            bias = jnp.broadcast_to(g.bias[pl.ds(channel, 1), :], (64, 256))
+            proj = jnp.broadcast_to(g.proj[pl.ds(channel, 1), :], (64, 256))
+            pre = conv[rows] + cells[rows] + bias
+            cdf = 0.5 * (1.0 + lax.erf(pre * math.sqrt(0.5)))
+            pdf = jnp.exp(-0.5 * pre * pre) * (1.0 / math.sqrt(TWO_PI))
+            grad = (proj * g.cot[...]) * (cdf + pre * pdf)
+            rounded.append(grad.astype(bf16))
+            second.snd1[slot, 64 * ch : 64 * ch + 64] = rounded[ch]
+            at = pl.ds(aligned(channel * 8, 8), 8)
+            g.bias_rows[at, :] = jnp.sum(grad.reshape(8, 8, 256), axis=0)
+            g.proj_rows[at, :] = jnp.sum(((pre * cdf) * g.cot[...]).reshape(8, 8, 256), axis=0)
+        if not isinstance(d, int):
+            back_start(n_col - d)
+        place(slot, jnp.concatenate(rounded, axis=0).astype(f32))
+
+    to_grid(first, lambda: first_fill(first), lambda: rest_of_conv(first), activate)
 
     piece = 80 // owners
 
     def cover_grad():
-        row_copies = send_halo_rows(second)
-        g.sums[0:32] = bias_sum
-        g.sums[32:64] = proj_sum
+        regroup(second)
+        of_channel = (lax.broadcasted_iota(jnp.int32, (32, 256), 1) // 8) == lax.broadcasted_iota(
+            jnp.int32, (32, 256), 0
+        )
+        gather = jnp.where(of_channel, 1.0, 0.0)
+        for at, rows in ((0, g.bias_rows), (32, g.proj_rows)):
+            g.sums[at : at + 32] = lax.dot_general(
+                gather, rows[...], NN, precision=HIGH, preferred_element_type=f32
+            )
         g.sums[64:128] = jnp.zeros((64, 256), f32)
         g.outer[...] = jnp.zeros_like(g.outer)
 
@@ -498,7 +518,6 @@
             g.outer[...] += dot(rows, grads, NT)
 
         loop(8, block)
-        copies = widen(second, row_copies)
         lane = lax.broadcasted_iota(jnp.int32, (96, 128), 1)
         taps = []
         for a in range(3):
@@ -522,9 +541,6 @@
                 push(g.part.at[t], g.got_row.at[row_at], g.row_s.at[t], g.row_r.at[row_at], "row", t).start()
 
         spread_taps(second, True)
-        for copy in copies:
-            copy.wait_recv()
-        fill_wide(second, 0, HALF_FILL)
 
     def sum_rows():
         @pl.when(row_at < owners)
@@ -560,7 +576,18 @@
 
             each(n_row, send)
 
-    to_modes(second, lambda i: second.snd1.at[i], cover_grad, sum_rows)
+    def cover_rows_back():
+        widen_now(second)
+        sum_rows()
+
+    def cover_rows_out():
+        first_fill(second)
+        sum_cols()
+
+    def write_out(slot, cells, d):
+        out_ref[pl.ds(aligned(slot * 256, 256), 256), :] = placed(slot) + cells
+
+    to_modes(second, lambda i: second.snd1.at[i], True, cover_grad, cover_rows_back)
     own_mode = lax.broadcasted_iota(jnp.int32, (256, 128), 0) & 3
     second.modes[...] = second.modes[...] * jnp.where(row_at * 4 + own_mode == 0, 1.0, 2.0)
     for kl in range(4):
@@ -577,16 +604,10 @@
             return carry
 
         lax.fori_loop(0, 32, one_channel, 0)
-    to_grid(second, sum_cols, lambda: rest_of_conv(second))
-
-    def finish(x):
-        put_grid_row(x, g.cells[pl.ds(aligned(x * 32, 32), 32), :] + grid_row(x))
+    to_grid(second, cover_rows_out, lambda: rest_of_conv(second), write_out)
 
     modes_ref[0] = first.modes[...]
     modes_ref[1] = second.modes[...]
-    loop(64, finish)
-    for i in range(n_col):
-        out_ref[256 * i : 256 * i + 256] = placed(i)
     for t in range(owners):
 
         @pl.when(row_at != t)

time: 163 us -> 137 us (0.84)
  Pallas kernels: 162 us -> 136 us
    pallas_call x1, Pallas kernels: 155 us -> 130 us  [per_device(): pl.pallas_call(functools.partial(step_kernel, n_row, n_col, owners), out_...]
where the time goes in v4:
time: 137 us
  Pallas kernels  136 us (99%)
    pallas_call x1, Pallas kernels, per_device(): pl.pallas_call(functools.partial(step_kernel, n_row, n_col, owners), out_...  130 us
    pallas_call x1, Pallas kernels, per_device(): pl.pallas_call(outputs_kernel, grid=(8,), out_shape=[jax.ShapeDtypeStruct...  6.75 us

profile of v4, /device:TPU:1, one launch (start us, length us, event | category | flops | bytes accessed | tf_op | source)
XLA Modules:
  0.0 137.0 jit_solution(17366523535242056651)
XLA Ops:
  0.6 129.6 %layer_step.1 = (f32[2048,256]{1,0:T(8,128)}, f32[2,256,128]{2,1,0:T(8,128)}, f32[80,128]{1,0:T(8,128)}) custom-call(bf16[8,256,256]{2,1,0:T(8,128)(2,1)} %bitcast.9, bf16[64,256]{1,0:T(8,128)(2,1)} %refs_1_.1, bf16[288,32]{1,0:T(8,128)(2,1)} %bitcast.11, f32[1,32]{1,0:T(1,128)} %bitcast.12, f32[1,32]{1,0:T(1,128)} %bitcast.13, ...), custom_call_target="tpu_custom_call" | custom-call | tf_op jit(solution)/shard_map/layer_step/pallas_call | solution.py:664
  130.2 6.8 %layer_outputs.1 = (f32[2048,256]{1,0:T(8,128)}, f32[4,2,32,32,32]{4,3,2,1,0:T(8,128)}, f32[288,32]{1,0:T(8,128)}, f32[1,32]{1,0:T(1,128)}, f32[1,32]{1,0:T(1,128)}) custom-call(f32[2048,256]{1,0:T(8,128)} %get-tuple-element.13.cells_ref, f32[512,128]{1,0:T(8,128)} %bitcast.10, f32[80,128]{1,0:T(8,128)} %get-tuple-element.15.small_ref), custom_call_target="tpu_custom_call" | custom-call | tf_op jit(solution)/shard_map/layer_outputs/pallas_call | solution.py:689

commit v5 on v4

--- a/solution.py
+++ b/solution.py
@@ -41,53 +41,6 @@
     return lax.dot_general(a, b, dims, preferred_element_type=jnp.float32)
 
 
-def exchange(axis, me, size, source, target, send_sem, recv_sem):
-    def copy(step, peer, slot):
-        return pltpu.make_async_remote_copy(
-            src_ref=source(peer),
-            dst_ref=target(slot),
-            send_sem=send_sem.at[step],
-            recv_sem=recv_sem.at[step],
-            device_id={axis: peer},
-            device_id_type=pl.DeviceIdType.MESH,
-        )
-
-    def start(step):
-        copy(step, lax.rem(me + step, size), me).start()
-
-    def wait_send(step):
-        copy(step, lax.rem(me + step, size), me).wait_send()
-
-    def wait_recv(step):
-        origin = lax.rem(me + size - step, size)
-        copy(step, lax.rem(me + step, size), origin).wait_recv()
-        return origin
-
-    return start, wait_send, wait_recv
-
-
-def each(size, body):
-    def step(index, carry):
-        body(index)
-        return carry
-
-    lax.fori_loop(1, size, step, 0)
-
-
-def part_swap(value, sign):
-    rows = value.shape[0]
-    is_real = (lax.broadcasted_iota(jnp.int32, value.shape, 0) & 4) == 0
-    after = pltpu.roll(value, rows - 4, 0)
-    before = pltpu.roll(value, 4, 0)
-    return jnp.where(is_real, sign * after, -sign * before)
-
-
-class Group:
-    def __init__(self, names, refs):
-        for name, ref in zip(names, refs):
-            setattr(self, name, ref)
-
-
 def push(src, dst, send_sem, recv_sem, axis, peer):
     return pltpu.make_async_remote_copy(
         src_ref=src,
@@ -97,6 +50,63 @@
         device_id={axis: peer},
         device_id_type=pl.DeviceIdType.MESH,
     )
+
+
+class Exchange:
+    def __init__(self, axis, me, size, source, slots, send_sem, recv_sem, shared):
+        (self.axis, self.me, self.size, self.source, self.slots) = (axis, me, size, source, slots)
+        (self.send_sem, self.recv_sem, self.shared) = (send_sem, recv_sem, shared)
+
+    def peer(self, step):
+        return (self.me + step) & (self.size - 1)
+
+    def copy(self, step, src, dst, peer):
+        recv_sem = self.recv_sem if self.shared else self.recv_sem.at[step]
+        return push(src, dst, self.send_sem, recv_sem, self.axis, peer)
+
+    def start(self, step):
+        peer = self.peer(step)
+        self.copy(step, self.source(peer), self.slots.at[self.me], peer).start()
+
+    def start_all(self):
+        each(self.size, self.start)
+
+    def take(self, step):
+        origin = (self.me - step) & (self.size - 1)
+        self.copy(step, self.slots.at[origin], self.slots.at[origin], origin).wait_recv()
+        return origin
+
+    def every(self):
+        rest = self.slots.at[pl.ds(0, self.size - 1)]
+        return self.copy(1, rest, rest, self.peer(1))
+
+    def take_all(self):
+        self.every().wait_recv()
+
+    def sent(self):
+        self.every().wait_send()
+
+
+def each(size, body):
+    def step(index, carry):
+        body(index)
+        return carry
+
+    lax.fori_loop(1, size, step, 0)
+
+
+def part_swap(value, sign):
+    rows = value.shape[0]
+    is_real = (lax.broadcasted_iota(jnp.int32, value.shape, 0) & 4) == 0
+    after = pltpu.roll(value, rows - 4, 0)
+    before = pltpu.roll(value, 4, 0)
+    return jnp.where(is_real, sign * after, -sign * before)
+
+
+class Group:
+    def __init__(self, names, refs):
+        for name, ref in zip(names, refs):
+            setattr(self, name, ref)
 
 
 def aligned(value, to):
@@ -133,8 +143,8 @@
         er=dma((2,)),
     )
     for step, size in ((1, n_col), (3, n_row), (5, n_col), (7, n_col), (9, n_row), (10, n_col)):
-        found["s%d" % step] = dma((size,))
-        found["r%d" % step] = dma((size,))
+        found["s%d" % step] = dma
+        found["r%d" % step] = dma((size,)) if step in (1, 10) else dma
     return found
 
 
@@ -153,6 +163,8 @@
         bias_rows=pltpu.VMEM((256, 256), f32),
         proj_rows=pltpu.VMEM((256, 256), f32),
         cot=pltpu.VMEM((64, 256), f32),
+        out=pltpu.VMEM((2048, 256), f32),
+        out_s=dma,
         acc=pltpu.VMEM((8 * n_row, 256), f32),
         rows_x=pltpu.VMEM((32, nx), bf16),
         mix=pltpu.VMEM((256, 128), f32),
@@ -166,10 +178,10 @@
         got_all=pltpu.VMEM((owners, piece, 128), f32),
         load=dma((4,)),
         row_s=dma((owners,)),
-        row_r=dma((n_row,)),
-        col_s=dma((n_col,)),
-        col_r=dma((n_col,)),
-        all_s=dma((n_row,)),
+        row_r=dma,
+        col_s=dma,
+        col_r=dma,
+        all_s=dma,
         all_r=dma((owners,)),
     )
 
@@ -198,9 +210,9 @@
         load.start()
     barrier = pltpu.get_barrier_semaphore()
     each(n_col, lambda d: pl.semaphore_signal(
-        barrier, inc=1, device_id={"col": lax.rem(col_at + d, n_col)}, device_id_type=pl.DeviceIdType.MESH))
+        barrier, inc=1, device_id={"col": (col_at + d) & (n_col - 1)}, device_id_type=pl.DeviceIdType.MESH))
     each(n_row, lambda d: pl.semaphore_signal(
-        barrier, inc=1, device_id={"row": lax.rem(row_at + d, n_row)}, device_id_type=pl.DeviceIdType.MESH))
+        barrier, inc=1, device_id={"row": (row_at + d) & (n_row - 1)}, device_id_type=pl.DeviceIdType.MESH))
     pl.semaphore_wait(barrier, n_col - 1 + n_row - 1)
 
     def loop(size, body):
@@ -292,16 +304,16 @@
     def to_modes(p, source, started, cover, cover_rows):
         own = pltpu.make_async_copy(source(col_at), p.buf1.at[col_at], p.own)
         own.start()
-        start, sent, got = exchange("col", col_at, n_col, source, lambda i: p.buf1.at[i], p.s1, p.r1)
+        fields = Exchange("col", col_at, n_col, source, p.buf1, p.s1, p.r1, False)
         if not started:
-            each(n_col, start)
-        pending.append(lambda: each(n_col, sent))
+            fields.start_all()
+        pending.append(fields.sent)
         cover()
         own.wait()
         g.acc[...] = dot(g.ty[col_at], p.buf1[col_at], NT)
 
         def add_block(d):
-            origin = got(d)
+            origin = fields.take(d)
             g.acc[...] += dot(g.ty[origin], p.buf1[origin], NT)
 
         each(n_col, add_block)
@@ -309,12 +321,12 @@
         upper = whole[:, :128].reshape(n_row, 8, 128)
         lower = whole[:, 128:].reshape(n_row, 8, 128)
         p.snd3[...] = jnp.concatenate([upper, lower], axis=1).astype(bf16)
-        start3, sent3, got3 = exchange("row", row_at, n_row, lambda i: p.snd3.at[i], lambda i: p.rcv3.at[i], p.s3, p.r3)
-        each(n_row, start3)
-        pending.append(lambda: each(n_row, sent3))
+        rows = Exchange("row", row_at, n_row, lambda i: p.snd3.at[i], p.rcv3, p.s3, p.r3, True)
+        rows.start_all()
+        pending.append(rows.sent)
         p.rcv3[row_at] = p.snd3[row_at]
         cover_rows()
-        each(n_row, got3)
+        rows.take_all()
         for s in range(pairs):
             one = p.rcv3[2 * s].astype(f32)
             two = p.rcv3[2 * s + 1].astype(f32)
@@ -327,14 +339,12 @@
         coeffs = jnp.concatenate([coeffs[0:8], coeffs[16:24], coeffs[8:16], coeffs[24:32]], axis=0)
         p.snd5[0] = coeffs[:, :128].astype(bf16)
         p.snd5[1] = coeffs[:, 128:].astype(bf16)
-        start5, sent5, got5 = exchange(
-            "col", col_at, n_col, lambda i: p.snd5.at[i // 4], lambda i: p.rcv5.at[i], p.s5, p.r5
-        )
-        each(n_col, start5)
-        pending.append(lambda: each(n_col, sent5))
+        parts = Exchange("col", col_at, n_col, lambda i: p.snd5.at[i // 4], p.rcv5, p.s5, p.r5, True)
+        parts.start_all()
+        pending.append(parts.sent)
         p.rcv5[col_at] = p.snd5[col_at // 4]
         g.mix[...] = jnp.zeros_like(g.mix)
-        each(n_col, got5)
+        parts.take_all()
         for i in range(n_col):
             p.modes[32 * i : 32 * i + 32] = pltpu.roll(p.rcv5[i].astype(f32), back_shift, 1)
 
@@ -347,11 +357,11 @@
                 p.snd7[i, 16 * odd_channel : 16 * odd_channel + 16] = jnp.concatenate(
                     [upper, lower], axis=0
                 ).astype(bf16)
-        start7, sent7, got7 = exchange("col", col_at, n_col, lambda i: p.snd7.at[i], lambda i: p.rcv7.at[i], p.s7, p.r7)
-        each(n_col, start7)
-        pending.append(lambda: each(n_col, sent7))
+        parts = Exchange("col", col_at, n_col, lambda i: p.snd7.at[i], p.rcv7, p.s7, p.r7, True)
+        parts.start_all()
+        pending.append(parts.sent)
         p.rcv7[col_at] = p.snd7[col_at]
-        each(n_col, got7)
+        parts.take_all()
         halves = [sum(p.rcv7[4 * h + q].astype(f32) for q in range(4)) for h in range(2)]
         mixed = jnp.concatenate(halves, axis=1)
         swapped = part_swap(mixed, -1.0)
@@ -362,33 +372,31 @@
             odd = by_rows[16:32, 128 * s : 128 * s + 128]
             p.snd9[2 * s] = jnp.where(low, even, pltpu.roll(odd, 64, 1)).astype(bf16)
             p.snd9[2 * s + 1] = jnp.where(low, pltpu.roll(even, 64, 1), odd).astype(bf16)
-        start9, sent9, got9 = exchange("row", row_at, n_row, lambda i: p.snd9.at[i], lambda i: p.rcv9.at[i], p.s9, p.r9)
-        each(n_row, start9)
-        pending.append(lambda: each(n_row, sent9))
+        rows = Exchange("row", row_at, n_row, lambda i: p.snd9.at[i], p.rcv9, p.s9, p.r9, True)
+        rows.start_all()
+        pending.append(rows.sent)
         p.rcv9[row_at] = p.snd9[row_at]
         cover_rows()
-        each(n_row, got9)
+        rows.take_all()
         got = p.rcv9[...].astype(f32)
         own_rows = jnp.concatenate(
             [got[:, :8].reshape(8 * n_row, 128), got[:, 8:].reshape(8 * n_row, 128)], axis=1
         )
         lhs = jnp.transpose(own_rows).astype(bf16)
-        start10, sent10, got10 = exchange(
-            "col", col_at, n_col, lambda i: p.snd10.at[i], lambda i: p.rcv10.at[i], p.s10, p.r10
-        )
+        cells = Exchange("col", col_at, n_col, lambda i: p.snd10.at[i], p.rcv10, p.s10, p.r10, False)
 
         def make_cells(d):
-            peer = lax.rem(col_at + d, n_col)
+            peer = cells.peer(d)
             p.snd10[peer] = dot(lhs, g.ty[peer], NN).astype(bf16)
-            start10(d)
+            cells.start(d)
 
         each(n_col, make_cells)
-        pending.append(lambda: each(n_col, sent10))
+        pending.append(cells.sent)
         cover_cells()
         use(col_at, dot(lhs, g.ty[col_at], NN), 0)
 
         def take(d):
-            origin = got10(d)
+            origin = cells.take(d)
             use(origin, p.rcv10[origin].astype(f32), d)
 
         each(n_col, take)
@@ -470,9 +478,7 @@
         g.mix[32 * kl : 32 * kl + 32, 0:32] = real.astype(bf16).astype(f32) * factor
         g.mix[128 + 32 * kl : 160 + 32 * kl, 0:32] = imag.astype(bf16).astype(f32) * factor
 
-    back_start, _, _ = exchange(
-        "col", col_at, n_col, lambda i: second.snd1.at[i], lambda i: second.buf1.at[i], second.s1, second.r1
-    )
+    back = Exchange("col", col_at, n_col, lambda i: second.snd1.at[i], second.buf1, second.s1, second.r1, False)
 
     def activate(slot, cells, d):
         conv = placed(slot)
@@ -492,7 +498,7 @@
             g.bias_rows[at, :] = jnp.sum(grad.reshape(8, 8, 256), axis=0)
             g.proj_rows[at, :] = jnp.sum(((pre * cdf) * g.cot[...]).reshape(8, 8, 256), axis=0)
         if not isinstance(d, int):
-            back_start(n_col - d)
+            back.start(n_col - d)
         place(slot, jnp.concatenate(rounded, axis=0).astype(f32))
 
     to_grid(first, lambda: first_fill(first), lambda: rest_of_conv(first), activate)
@@ -538,7 +544,7 @@
 
             @pl.when(row_at != t)
             def _():
-                push(g.part.at[t], g.got_row.at[row_at], g.row_s.at[t], g.row_r.at[row_at], "row", t).start()
+                push(g.part.at[t], g.got_row.at[row_at], g.row_s.at[t], g.row_r, "row", t).start()
 
         spread_taps(second, True)
 
@@ -546,33 +552,23 @@
         @pl.when(row_at < owners)
         def _():
             g.got_row[row_at] = g.part[row_at]
-
-            def wait(d):
-                origin = lax.rem(row_at + d, n_row)
-                push(g.part.at[0], g.got_row.at[origin], g.row_s.at[0], g.row_r.at[origin], "row", origin).wait_recv()
-
-            each(n_row, wait)
+            Exchange("row", row_at, n_row, None, g.got_row, g.row_s.at[0], g.row_r, True).take_all()
             g.sum_row[...] = jnp.sum(g.got_row[...], axis=0)
             g.got_col[col_at] = g.sum_row[...]
-            start, _, _ = exchange(
-                "col", col_at, n_col, lambda i: g.sum_row, lambda i: g.got_col.at[i], g.col_s, g.col_r
-            )
-            each(n_col, start)
+            Exchange("col", col_at, n_col, lambda i: g.sum_row, g.got_col, g.col_s, g.col_r, True).start_all()
 
     def sum_cols():
         @pl.when(row_at < owners)
         def _():
-            _, sent, got = exchange(
-                "col", col_at, n_col, lambda i: g.sum_row, lambda i: g.got_col.at[i], g.col_s, g.col_r
-            )
-            each(n_col, got)
-            each(n_col, sent)
+            sums = Exchange("col", col_at, n_col, lambda i: g.sum_row, g.got_col, g.col_s, g.col_r, True)
+            sums.take_all()
+            sums.sent()
             g.total[...] = jnp.sum(g.got_col[...], axis=0)
             g.got_all[row_at] = g.total[...]
 
             def send(d):
-                peer = lax.rem(row_at + d, n_row)
-                push(g.total, g.got_all.at[row_at], g.all_s.at[d], g.all_r.at[row_at], "row", peer).start()
+                peer = (row_at + d) & (n_row - 1)
+                push(g.total, g.got_all.at[row_at], g.all_s, g.all_r.at[row_at], "row", peer).start()
 
             each(n_row, send)
 
@@ -585,7 +581,9 @@
         sum_cols()
 
     def write_out(slot, cells, d):
-        out_ref[pl.ds(aligned(slot * 256, 256), 256), :] = placed(slot) + cells
+        at = pl.ds(aligned(slot * 256, 256), 256)
+        g.out[at, :] = placed(slot) + cells
+        pltpu.make_async_copy(g.out.at[at], out_ref.at[at], g.out_s).start()
 
     to_modes(second, lambda i: second.snd1.at[i], True, cover_grad, cover_rows_back)
     own_mode = lax.broadcasted_iota(jnp.int32, (256, 128), 0) & 3
@@ -618,37 +616,38 @@
 
     @pl.when(row_at < owners)
     def _():
-        def sent(d):
-            peer = lax.rem(row_at + d, n_row)
-            push(g.total, g.got_all.at[row_at], g.all_s.at[d], g.all_r.at[row_at], "row", peer).wait_send()
-
-        each(n_row, sent)
+        Exchange("row", row_at, n_row, None, g.got_row, g.all_s, g.row_r, True).sent()
 
     small_ref[...] = g.got_all[...].reshape(80, 128)
     for wait in pending:
         wait()
-
-
-def outputs_kernel(cells_ref, modes_ref, small_ref, out_ref, gspec_ref, conv_ref, bias_ref, proj_ref):
-    out_ref[...] = cells_ref[...]
-    kl = pl.program_id(0) // 2
-    first = lax.rem(pl.program_id(0), 2) * 16
-    g_re = modes_ref[pl.ds(256 + kl, 32, stride=8), :][:, :32]
-    g_im = modes_ref[pl.ds(260 + kl, 32, stride=8), :][:, :32]
-    for i in range(16):
-        s_re = modes_ref[pl.ds(8 * (first + i) + kl, 1), :][:, :32]
-        s_im = modes_ref[pl.ds(8 * (first + i) + 4 + kl, 1), :][:, :32]
-        gspec_ref[0, 0, i] = g_re * s_re + g_im * s_im
-        gspec_ref[0, 1, i] = g_im * s_re - g_re * s_im
-
-    @pl.when(pl.program_id(0) == 0)
-    def _():
-        for q in range(4):
-            rows = small_ref[0:72]
-            conv_ref[72 * q : 72 * q + 72] = (pltpu.roll(rows, 128 - 32 * q, 1) if q else rows)[:, :32]
-        rows = small_ref[72:80]
-        bias_ref[...] = rows[0:1, :32]
-        proj_ref[...] = pltpu.roll(rows, 96, 1)[0:1, :32]
+    pltpu.make_async_copy(g.out, out_ref, g.out_s).wait()
+
+
+def outputs_kernel(cells_ref, modes_ref, small_ref, out_ref, gspec_ref, conv_ref, bias_ref, proj_ref, weight, sems):
+    copies = []
+    for q in range(4):
+        at = pl.ds(512 * q, 512)
+        copies.append(pltpu.make_async_copy(cells_ref.at[at], out_ref.at[at], sems.at[q]))
+        copies[q].start()
+    for kl in range(4):
+        g_re = modes_ref[pl.ds(256 + kl, 32, stride=8), :][:, :32]
+        g_im = modes_ref[pl.ds(260 + kl, 32, stride=8), :][:, :32]
+        for i in range(32):
+            s_re = modes_ref[8 * i + kl : 8 * i + kl + 1, :][:, :32]
+            s_im = modes_ref[8 * i + 4 + kl : 8 * i + 5 + kl, :][:, :32]
+            weight[kl, 0, i] = g_re * s_re + g_im * s_im
+            weight[kl, 1, i] = g_im * s_re - g_re * s_im
+        copies.append(pltpu.make_async_copy(weight.at[kl], gspec_ref.at[kl], sems.at[4 + kl]))
+        copies[4 + kl].start()
+    for q in range(4):
+        rows = small_ref[0:72]
+        conv_ref[72 * q : 72 * q + 72] = (pltpu.roll(rows, 128 - 32 * q, 1) if q else rows)[:, :32]
+    rows = small_ref[72:80]
+    bias_ref[...] = rows[0:1, :32]
+    proj_ref[...] = pltpu.roll(rows, 96, 1)[0:1, :32]
+    for copy in copies:
+        copy.wait()
 
 
 def per_device(n_row, n_col, ocean_field, cotangent, conv_weight, conv_bias, projection, mode_weight):
@@ -669,7 +668,7 @@
             jax.ShapeDtypeStruct((80, 128), jnp.float32),
         ],
         in_specs=[hbm, vmem, vmem, vmem, vmem, hbm, hbm, hbm],
-        out_specs=[vmem, vmem, vmem],
+        out_specs=[hbm, vmem, vmem],
         scratch_shapes=scratch,
         compiler_params=pltpu.CompilerParams(
             collective_id=0, has_side_effects=True, vmem_limit_bytes=VMEM_BYTES
@@ -685,10 +684,8 @@
         ty,
         tx,
     )
-    whole = lambda *shape: pl.BlockSpec(shape, lambda t: (0,) * len(shape))
     grad_input, grad_spec, grad_conv, grad_bias, grad_proj = pl.pallas_call(
         outputs_kernel,
-        grid=(8,),
         out_shape=[
             jax.ShapeDtypeStruct((chans * rows_dev, cols_dev), jnp.float32),
             jax.ShapeDtypeStruct(mode_weight.shape, jnp.float32),
@@ -696,14 +693,9 @@
             jax.ShapeDtypeStruct((1, chans), jnp.float32),
             jax.ShapeDtypeStruct((1, chans), jnp.float32),
         ],
-        in_specs=[pl.BlockSpec((256, 256), lambda t: (t, 0)), whole(512, 128), whole(80, 128)],
-        out_specs=[
-            pl.BlockSpec((256, 256), lambda t: (t, 0)),
-            pl.BlockSpec((1, 2, 16, 32, 32), lambda t: (t // 2, 0, t % 2, 0, 0)),
-            whole(9 * chans, chans),
-            whole(1, chans),
-            whole(1, chans),
-        ],
+        in_specs=[hbm, vmem, vmem],
+        out_specs=[hbm, hbm, vmem, vmem, vmem],
+        scratch_shapes=[pltpu.VMEM(mode_weight.shape, jnp.float32), pltpu.SemaphoreType.DMA((8,))],
         compiler_params=pltpu.CompilerParams(vmem_limit_bytes=VMEM_BYTES),
         name="layer_outputs",
     )(cells, modes.reshape(512, 128), small)

time: 137 us -> 191 us (1.39)
  Pallas kernels: 136 us -> 190 us
    pallas_call x1, Pallas kernels: 6.75 us -> 66.3 us  [per_device(): pl.pallas_call(outputs_kernel, out_shape=[jax.ShapeDtypeStruct((chans * r...]
    pallas_call x1, Pallas kernels: 130 us -> 124 us  [per_device(): pl.pallas_call(functools.partial(step_kernel, n_row, n_col, owners), out_...]
where the time goes in v5:
time: 191 us
  Pallas kernels  190 us (99%)
    pallas_call x1, Pallas kernels, per_device(): pl.pallas_call(functools.partial(step_kernel, n_row, n_col, owners), out_...  124 us
    pallas_call x1, Pallas kernels, per_device(): pl.pallas_call(outputs_kernel, out_shape=[jax.ShapeDtypeStruct((chans * r...  66.3 us

profile of v5, /device:TPU:1, one launch (start us, length us, event | category | flops | bytes accessed | tf_op | source)
XLA Modules:
  0.0 191.0 jit_solution(7242344074413687863)
XLA Ops:
  0.6 124.1 %layer_step.1 = (f32[2048,256]{1,0:T(8,128)}, f32[2,256,128]{2,1,0:T(8,128)}, f32[80,128]{1,0:T(8,128)}) custom-call(bf16[8,256,256]{2,1,0:T(8,128)(2,1)} %bitcast.9, bf16[64,256]{1,0:T(8,128)(2,1)} %refs_1_.1, bf16[288,32]{1,0:T(8,128)(2,1)} %bitcast.11, f32[1,32]{1,0:T(1,128)} %bitcast.12, f32[1,32]{1,0:T(1,128)} %bitcast.13, ...), custom_call_target="tpu_custom_call" | custom-call | tf_op jit(solution)/shard_map/layer_step/pallas_call | solution.py:663
  124.7 66.3 %layer_outputs.1 = (f32[2048,256]{1,0:T(8,128)}, f32[4,2,32,32,32]{4,3,2,1,0:T(8,128)}, f32[288,32]{1,0:T(8,128)}, f32[1,32]{1,0:T(1,128)}, f32[1,32]{1,0:T(1,128)}) custom-call(f32[2048,256]{1,0:T(8,128)} %get-tuple-element.13.cells_ref, f32[512,128]{1,0:T(8,128)} %bitcast.10, f32[80,128]{1,0:T(8,128)} %get-tuple-element.15.small_ref), custom_call_target="tpu_custom_call" | custom-call | tf_op jit(solution)/shard_map/layer_outputs/pallas_call | solution.py:687

commit v6 on v5

--- a/solution.py
+++ b/solution.py
@@ -624,12 +624,13 @@
     pltpu.make_async_copy(g.out, out_ref, g.out_s).wait()
 
 
-def outputs_kernel(cells_ref, modes_ref, small_ref, out_ref, gspec_ref, conv_ref, bias_ref, proj_ref, weight, sems):
+def outputs_kernel(cells_ref, modes_ref, small_ref, out_ref, gspec_ref, conv_ref, bias_ref, proj_ref, weight, cells, sems):
     copies = []
-    for q in range(4):
-        at = pl.ds(512 * q, 512)
-        copies.append(pltpu.make_async_copy(cells_ref.at[at], out_ref.at[at], sems.at[q]))
-        copies[q].start()
+    loads = []
+    parts = [pl.ds(512 * q, 512) for q in range(4)]
+    for q, at in enumerate(parts):
+        loads.append(pltpu.make_async_copy(cells_ref.at[at], cells.at[at], sems.at[q]))
+        loads[q].start()
     for kl in range(4):
         g_re = modes_ref[pl.ds(256 + kl, 32, stride=8), :][:, :32]
         g_im = modes_ref[pl.ds(260 + kl, 32, stride=8), :][:, :32]
@@ -639,7 +640,10 @@
             weight[kl, 0, i] = g_re * s_re + g_im * s_im
             weight[kl, 1, i] = g_im * s_re - g_re * s_im
         copies.append(pltpu.make_async_copy(weight.at[kl], gspec_ref.at[kl], sems.at[4 + kl]))
-        copies[4 + kl].start()
+        copies[-1].start()
+        loads[kl].wait()
+        copies.append(pltpu.make_async_copy(cells.at[parts[kl]], out_ref.at[parts[kl]], sems.at[8 + kl]))
+        copies[-1].start()
     for q in range(4):
         rows = small_ref[0:72]
         conv_ref[72 * q : 72 * q + 72] = (pltpu.roll(rows, 128 - 32 * q, 1) if q else rows)[:, :32]
@@ -695,7 +699,11 @@
         ],
         in_specs=[hbm, vmem, vmem],
         out_specs=[hbm, hbm, vmem, vmem, vmem],
-        scratch_shapes=[pltpu.VMEM(mode_weight.shape, jnp.float32), pltpu.SemaphoreType.DMA((8,))],
+        scratch_shapes=[
+            pltpu.VMEM(mode_weight.shape, jnp.float32),
+            pltpu.VMEM((chans * rows_dev, cols_dev), jnp.float32),
+            pltpu.SemaphoreType.DMA((12,)),
+        ],
         compiler_params=pltpu.CompilerParams(vmem_limit_bytes=VMEM_BYTES),
         name="layer_outputs",
     )(cells, modes.reshape(512, 128), small)

time: 191 us -> 130 us (0.68)
  Pallas kernels: 190 us -> 129 us
    pallas_call x1, Pallas kernels: 66.3 us -> 5.18 us  [per_device(): pl.pallas_call(outputs_kernel, out_shape=[jax.ShapeDtypeStruct((chans * r...]
where the time goes in v6:
time: 130 us
  Pallas kernels  129 us (99%)
    pallas_call x1, Pallas kernels, per_device(): pl.pallas_call(functools.partial(step_kernel, n_row, n_col, owners), out_...  124 us
    pallas_call x1, Pallas kernels, per_device(): pl.pallas_call(outputs_kernel, out_shape=[jax.ShapeDtypeStruct((chans * r...  5.18 us

profile of v6, /device:TPU:1, one launch (start us, length us, event | category | flops | bytes accessed | tf_op | source)
XLA Modules:
  0.0 129.9 jit_solution(4870850206114254793)
XLA Ops:
  0.6 124.1 %layer_step.1 = (f32[2048,256]{1,0:T(8,128)}, f32[2,256,128]{2,1,0:T(8,128)}, f32[80,128]{1,0:T(8,128)}) custom-call(bf16[8,256,256]{2,1,0:T(8,128)(2,1)} %bitcast.9, bf16[64,256]{1,0:T(8,128)(2,1)} %refs_1_.1, bf16[288,32]{1,0:T(8,128)(2,1)} %bitcast.11, f32[1,32]{1,0:T(1,128)} %bitcast.12, f32[1,32]{1,0:T(1,128)} %bitcast.13, ...), custom_call_target="tpu_custom_call" | custom-call | tf_op jit(solution)/shard_map/layer_step/pallas_call | solution.py:667
  124.7 5.2 %layer_outputs.1 = (f32[2048,256]{1,0:T(8,128)}, f32[4,2,32,32,32]{4,3,2,1,0:T(8,128)}, f32[288,32]{1,0:T(8,128)}, f32[1,32]{1,0:T(1,128)}, f32[1,32]{1,0:T(1,128)}) custom-call(f32[2048,256]{1,0:T(8,128)} %get-tuple-element.13.cells_ref, f32[512,128]{1,0:T(8,128)} %bitcast.10, f32[80,128]{1,0:T(8,128)} %get-tuple-element.15.small_ref), custom_call_target="tpu_custom_call" | custom-call | tf_op jit(solution)/shard_map/layer_outputs/pallas_call | solution.py:691

commit v7 on v6

--- a/solution.py
+++ b/solution.py
@@ -124,6 +124,7 @@
         snd5=pltpu.VMEM((2, 32, 128), bf16),
         rcv5=pltpu.VMEM((n_col, 32, 128), bf16),
         modes=pltpu.VMEM((256, 128), f32),
+        flat=pltpu.VMEM((64, 128), f32),
         snd7=pltpu.VMEM((n_col, 32, 128), bf16),
         rcv7=pltpu.VMEM((n_col, 32, 128), bf16),
         snd9=pltpu.VMEM((n_row, 16, 128), bf16),
@@ -168,6 +169,8 @@
         acc=pltpu.VMEM((8 * n_row, 256), f32),
         rows_x=pltpu.VMEM((32, nx), bf16),
         mix=pltpu.VMEM((256, 128), f32),
+        packed=pltpu.VMEM((2, 32, 32, 128), f32),
+        mixed_back=pltpu.VMEM((64, 128), f32),
         outer=pltpu.VMEM((960, 256), f32),
         sums=pltpu.VMEM((128, 256), f32),
         part=pltpu.VMEM((owners, piece, 128), f32),
@@ -343,13 +346,11 @@
         parts.start_all()
         pending.append(parts.sent)
         p.rcv5[col_at] = p.snd5[col_at // 4]
-        g.mix[...] = jnp.zeros_like(g.mix)
         parts.take_all()
         for i in range(n_col):
             p.modes[32 * i : 32 * i + 32] = pltpu.roll(p.rcv5[i].astype(f32), back_shift, 1)
 
     def to_grid(p, cover_rows, cover_cells, use):
-        g.mix[...] = pltpu.roll(g.mix[...], quarter, 1)
         for i in range(n_col):
             for odd_channel in range(2):
                 upper = g.mix[pl.ds(4 * i + odd_channel, 8, stride=32), :]
@@ -442,6 +443,25 @@
     quarter = lax.rem(col_at, 4) * 32
     back_shift = lax.rem(128 - quarter, 128)
 
+    def flatten_modes(p):
+        for part in range(2):
+            p.flat[32 * part : 32 * part + 32] = jnp.concatenate(
+                [p.modes[pl.ds(4 * part + kl, 32, stride=8), :][:, :32] for kl in range(4)], axis=1
+            )
+
+    def pack_weight(i):
+        for part in range(2):
+            g.packed[part, i] = jnp.concatenate([g.weight[kl, part, i].astype(f32) for kl in range(4)], axis=1)
+
+    def spread_mix(parts):
+        lane = lax.broadcasted_iota(jnp.int32, (32, 128), 1)
+        mine = (lane >= quarter) & (lane < quarter + 32)
+        for part, value in enumerate(parts):
+            for kl in range(4):
+                moved = pltpu.roll(value, (quarter + 128 - 32 * kl) & 127, 1)
+                at = 128 * part + 32 * kl
+                g.mix[at : at + 32, :] = jnp.where(mine, moved, 0.0)
+
     def cover_field():
         loads[0].wait()
         for i in range(n_col):
@@ -452,6 +472,8 @@
         spread_taps(first, False)
         g.bias[...] = column(bias_ref)
         g.proj[...] = column(proj_ref)
+        loads[3].wait()
+        loop(32, pack_weight)
         loads[1].wait()
         loads[2].wait()
 
@@ -461,22 +483,21 @@
         return jnp.broadcast_to(value, (32, 256))
 
     to_modes(first, lambda i: v_ref.at[i], False, cover_field, lambda: widen_now(first))
-    loads[3].wait()
-    for kl in range(4):
-
-        def add_channel(i, sums):
-            real, imag = sums
-            s_re = first.modes[pl.ds(8 * i + kl, 1), :][:, :32]
-            s_im = first.modes[pl.ds(8 * i + 4 + kl, 1), :][:, :32]
-            w_re = g.weight[kl, 0, i].astype(f32)
-            w_im = g.weight[kl, 1, i].astype(f32)
-            return (real + (w_re * s_re - w_im * s_im), imag + (w_re * s_im + w_im * s_re))
-
-        zero = jnp.zeros((32, 32), f32)
-        real, imag = lax.fori_loop(0, 32, add_channel, (zero, zero))
-        factor = jnp.where(row_at * 4 + kl == 0, 1.0, 2.0).astype(f32) * scale
-        g.mix[32 * kl : 32 * kl + 32, 0:32] = real.astype(bf16).astype(f32) * factor
-        g.mix[128 + 32 * kl : 160 + 32 * kl, 0:32] = imag.astype(bf16).astype(f32) * factor
+    flatten_modes(first)
+
+    def add_channel(i, sums):
+        real, imag = sums
+        s_re = first.flat[pl.ds(i, 1), :]
+        s_im = first.flat[pl.ds(32 + i, 1), :]
+        w_re = g.packed[0, i]
+        w_im = g.packed[1, i]
+        return (real + (w_re * s_re - w_im * s_im), imag + (w_re * s_im + w_im * s_re))
+
+    zero = jnp.zeros((32, 128), f32)
+    real, imag = lax.fori_loop(0, 32, add_channel, (zero, zero))
+    frequency = row_at * 4 + lax.broadcasted_iota(jnp.int32, (32, 128), 1) // 32
+    factor = jnp.where(frequency == 0, 1.0, 2.0) * scale
+    spread_mix([value.astype(bf16).astype(f32) * factor for value in (real, imag)])
 
     back = Exchange("col", col_at, n_col, lambda i: second.snd1.at[i], second.buf1, second.s1, second.r1, False)
 
@@ -588,20 +609,18 @@
     to_modes(second, lambda i: second.snd1.at[i], True, cover_grad, cover_rows_back)
     own_mode = lax.broadcasted_iota(jnp.int32, (256, 128), 0) & 3
     second.modes[...] = second.modes[...] * jnp.where(row_at * 4 + own_mode == 0, 1.0, 2.0)
-    for kl in range(4):
-        g_re = second.modes[pl.ds(kl, 32, stride=8), :][:, :32]
-        g_im = second.modes[pl.ds(4 + kl, 32, stride=8), :][:, :32]
-
-        def one_channel(i, carry):
-            w_re = g.weight[kl, 0, i].astype(f32)
-            w_im = g.weight[kl, 1, i].astype(f32)
-            b_re = jnp.sum(w_re * g_re + w_im * g_im, axis=0, keepdims=True)
-            b_im = jnp.sum(w_re * g_im - w_im * g_re, axis=0, keepdims=True)
-            g.mix[pl.ds(32 * kl + i, 1), 0:32] = b_re.astype(bf16).astype(f32) * scale
-            g.mix[pl.ds(128 + 32 * kl + i, 1), 0:32] = b_im.astype(bf16).astype(f32) * scale
-            return carry
-
-        lax.fori_loop(0, 32, one_channel, 0)
+    flatten_modes(second)
+    g_re = second.flat[0:32]
+    g_im = second.flat[32:64]
+
+    def one_channel(i):
+        w_re = g.packed[0, i]
+        w_im = g.packed[1, i]
+        g.mixed_back[pl.ds(i, 1), :] = jnp.sum(w_re * g_re + w_im * g_im, axis=0, keepdims=True)
+        g.mixed_back[pl.ds(32 + i, 1), :] = jnp.sum(w_re * g_im - w_im * g_re, axis=0, keepdims=True)
+
+    loop(32, one_channel)
+    spread_mix([g.mixed_back[32 * part : 32 * part + 32].astype(bf16).astype(f32) * scale for part in range(2)])
     to_grid(second, cover_rows_out, lambda: rest_of_conv(second), write_out)
 
     modes_ref[0] = first.modes[...]

time: 130 us -> 127 us (0.977)
  Pallas kernels: 129 us -> 126 us
    pallas_call x1, Pallas kernels: 124 us -> 121 us  [per_device(): pl.pallas_call(functools.partial(step_kernel, n_row, n_col, owners), out_...]
where the time goes in v7:
time: 127 us
  Pallas kernels  126 us (99%)
    pallas_call x1, Pallas kernels, per_device(): pl.pallas_call(functools.partial(step_kernel, n_row, n_col, owners), out_...  121 us
    pallas_call x1, Pallas kernels, per_device(): pl.pallas_call(outputs_kernel, out_shape=[jax.ShapeDtypeStruct((chans * r...  5.18 us

profile of v7, /device:TPU:1, one launch (start us, length us, event | category | flops | bytes accessed | tf_op | source)
XLA Modules:
  0.0 127.0 jit_solution(17409738754635782300)
XLA Ops:
  0.6 121.2 %layer_step.1 = (f32[2048,256]{1,0:T(8,128)}, f32[2,256,128]{2,1,0:T(8,128)}, f32[80,128]{1,0:T(8,128)}) custom-call(bf16[8,256,256]{2,1,0:T(8,128)(2,1)} %bitcast.9, bf16[64,256]{1,0:T(8,128)(2,1)} %refs_1_.1, bf16[288,32]{1,0:T(8,128)(2,1)} %bitcast.11, f32[1,32]{1,0:T(1,128)} %bitcast.12, f32[1,32]{1,0:T(1,128)} %bitcast.13, ...), custom_call_target="tpu_custom_call" | custom-call | tf_op jit(solution)/shard_map/layer_step/pallas_call | solution.py:686
  121.8 5.2 %layer_outputs.1 = (f32[2048,256]{1,0:T(8,128)}, f32[4,2,32,32,32]{4,3,2,1,0:T(8,128)}, f32[288,32]{1,0:T(8,128)}, f32[1,32]{1,0:T(1,128)}, f32[1,32]{1,0:T(1,128)}) custom-call(f32[2048,256]{1,0:T(8,128)} %get-tuple-element.13.cells_ref, f32[512,128]{1,0:T(8,128)} %bitcast.10, f32[80,128]{1,0:T(8,128)} %get-tuple-element.15.small_ref), custom_call_target="tpu_custom_call" | custom-call | tf_op jit(solution)/shard_map/layer_outputs/pallas_call | solution.py:710

commit v8 on v7

--- a/solution.py
+++ b/solution.py
@@ -69,7 +69,8 @@
         self.copy(step, self.source(peer), self.slots.at[self.me], peer).start()
 
     def start_all(self):
-        each(self.size, self.start)
+        for step in range(1, self.size):
+            self.start(step)
 
     def take(self, step):
         origin = (self.me - step) & (self.size - 1)
@@ -212,10 +213,11 @@
     for load in loads:
         load.start()
     barrier = pltpu.get_barrier_semaphore()
-    each(n_col, lambda d: pl.semaphore_signal(
-        barrier, inc=1, device_id={"col": (col_at + d) & (n_col - 1)}, device_id_type=pl.DeviceIdType.MESH))
-    each(n_row, lambda d: pl.semaphore_signal(
-        barrier, inc=1, device_id={"row": (row_at + d) & (n_row - 1)}, device_id_type=pl.DeviceIdType.MESH))
+    for axis, me, size in (("row", row_at, n_row), ("col", col_at, n_col)):
+        for d in range(1, size):
+            pl.semaphore_signal(
+                barrier, inc=1, device_id={axis: (me + d) & (size - 1)}, device_id_type=pl.DeviceIdType.MESH
+            )
     pl.semaphore_wait(barrier, n_col - 1 + n_row - 1)
 
     def loop(size, body):

time: 127 us -> 127 us (level)
  no operation moved by 1% of the time
where the time goes in v8:
time: 127 us
  Pallas kernels  127 us (100%)
    pallas_call x1, Pallas kernels, per_device(): pl.pallas_call(functools.partial(step_kernel, n_row, n_col, owners), out_...  121 us
    pallas_call x1, Pallas kernels, per_device(): pl.pallas_call(outputs_kernel, out_shape=[jax.ShapeDtypeStruct((chans * r...  5.18 us

profile of v8, /device:TPU:1, one launch (start us, length us, event | category | flops | bytes accessed | tf_op | source)
XLA Modules:
  0.0 127.2 jit_solution(14476278557550932210)
XLA Ops:
  0.6 121.4 %layer_step.1 = (f32[2048,256]{1,0:T(8,128)}, f32[2,256,128]{2,1,0:T(8,128)}, f32[80,128]{1,0:T(8,128)}) custom-call(bf16[8,256,256]{2,1,0:T(8,128)(2,1)} %bitcast.9, bf16[64,256]{1,0:T(8,128)(2,1)} %refs_1_.1, bf16[288,32]{1,0:T(8,128)(2,1)} %bitcast.11, f32[1,32]{1,0:T(1,128)} %bitcast.12, f32[1,32]{1,0:T(1,128)} %bitcast.13, ...), custom_call_target="tpu_custom_call" | custom-call | tf_op jit(solution)/shard_map/layer_step/pallas_call | solution.py:688
  122.0 5.2 %layer_outputs.1 = (f32[2048,256]{1,0:T(8,128)}, f32[4,2,32,32,32]{4,3,2,1,0:T(8,128)}, f32[288,32]{1,0:T(8,128)}, f32[1,32]{1,0:T(1,128)}, f32[1,32]{1,0:T(1,128)}) custom-call(f32[2048,256]{1,0:T(8,128)} %get-tuple-element.13.cells_ref, f32[512,128]{1,0:T(8,128)} %bitcast.10, f32[80,128]{1,0:T(8,128)} %get-tuple-element.15.small_ref), custom_call_target="tpu_custom_call" | custom-call | tf_op jit(solution)/shard_map/layer_outputs/pallas_call | solution.py:712

commit v9 on v7

--- a/solution.py
+++ b/solution.py
@@ -129,7 +129,6 @@
         rcv7=pltpu.VMEM((n_col, 32, 128), bf16),
         snd9=pltpu.VMEM((n_row, 16, 128), bf16),
         rcv9=pltpu.VMEM((n_row, 16, 128), bf16),
-        snd10=pltpu.VMEM((n_col, 256, 256), bf16),
         rcv10=pltpu.VMEM((n_col, 256, 256), bf16),
         raw=pltpu.VMEM((68 * 32, 256), bf16),
         halo=pltpu.VMEM((2, 32, 256), bf16),
@@ -144,8 +143,8 @@
         er=dma((2,)),
     )
     for step, size in ((1, n_col), (3, n_row), (5, n_col), (7, n_col), (9, n_row), (10, n_col)):
-        found["s%d" % step] = dma
-        found["r%d" % step] = dma((size,)) if step in (1, 10) else dma
+        found["s%d" % step] = dma((9,)) if step == 10 else dma
+        found["r%d" % step] = dma((9,)) if step == 10 else dma((size,)) if step == 1 else dma
     return found
 
 
@@ -295,14 +294,14 @@
         for x in range(8):
             p.taps[32 * x : 32 * x + 32, :] = (pltpu.roll(padded, 96 * x, 1) if x else padded).astype(bf16)
 
-    def convolve(p):
+    def convolve(p, start, stop):
         def block(t):
             rows = p.wide[pl.ds(aligned(t * 768, 16), 1024), :]
             result = dot(p.taps[...], rows, NN)
             for x in range(8):
                 put_grid_row(8 * t + x, result[32 * x : 32 * x + 32])
 
-        loop(8, block)
+        loop(stop - start, lambda t: block(t + start))
 
     def to_modes(p, source, started, cover, cover_rows):
         own = pltpu.make_async_copy(source(col_at), p.buf1.at[col_at], p.own)
@@ -384,23 +383,53 @@
             [got[:, :8].reshape(8 * n_row, 128), got[:, 8:].reshape(8 * n_row, 128)], axis=1
         )
         lhs = jnp.transpose(own_rows).astype(bf16)
-        cells = Exchange("col", col_at, n_col, lambda i: p.snd10.at[i], p.rcv10, p.s10, p.r10, False)
-
-        def make_cells(d):
-            peer = cells.peer(d)
-            p.snd10[peer] = dot(lhs, g.ty[peer], NN).astype(bf16)
-            cells.start(d)
-
-        each(n_col, make_cells)
-        pending.append(cells.sent)
-        cover_cells()
+        def at(dy, dz):
+            return ((((col_at >> 1) + dy) & (n_col // 2 - 1)) << 1) | ((col_at + dz) & 1)
+
+        ahead, behind, beside, far = (at(1, 0), at(n_col // 2 - 1, 0), at(0, 1), at(2, 0))
+        behind_beside, ahead_beside, far_beside = (at(n_col // 2 - 1, 1), at(1, 1), at(2, 1))
+
+        def send(kind, block, to, rows=None):
+            ref = p.rcv10.at[block] if rows is None else p.rcv10.at[block, pl.ds(128 * rows, 128)]
+            copy = push(ref, ref, p.s10.at[kind], p.r10.at[kind], "col", to)
+            copy.start()
+            pending.append(copy.wait_send)
+
+        def arrived(kind, block, rows=None):
+            ref = p.rcv10.at[block] if rows is None else p.rcv10.at[block, pl.ds(128 * rows, 128)]
+            push(ref, ref, p.s10.at[kind], p.r10.at[kind], "col", beside).wait_recv()
+
+        def give(block):
+            use(block, dot(p.rcv10[block], g.ty[col_at], NN), (col_at - block) & (n_col - 1))
+
+        p.rcv10[col_at] = lhs
+        send(0, col_at, ahead)
+        send(1, col_at, behind)
+        send(2, col_at, beside)
+        cover_cells[0]()
+        arrived(2, beside)
+        send(3, beside, ahead)
+        send(4, beside, behind)
+        arrived(0, behind)
+        send(5, behind, ahead, 0)
+        arrived(1, ahead)
+        send(6, ahead, behind, 1)
+        cover_cells[1]()
+        arrived(3, behind_beside)
+        send(7, behind_beside, ahead, 0)
+        arrived(4, ahead_beside)
+        send(8, ahead_beside, behind, 1)
+        cover_cells[2]()
         use(col_at, dot(lhs, g.ty[col_at], NN), 0)
-
-        def take(d):
-            origin = cells.take(d)
-            use(origin, p.rcv10[origin].astype(f32), d)
-
-        each(n_col, take)
+        ready = [beside, behind, ahead, behind_beside, ahead_beside]
+        for block in ready:
+            give(block)
+        arrived(5, far, 0)
+        arrived(6, far, 1)
+        give(far)
+        arrived(7, far_beside, 0)
+        arrived(8, far_beside, 1)
+        give(far_beside)
 
     def first_fill(p):
         for copy in p.edge_copies:
@@ -408,8 +437,7 @@
         fill_wide(p, 0, HALF_FILL)
 
     def rest_of_conv(p):
-        fill_wide(p, HALF_FILL, 17)
-        convolve(p)
+        return (lambda: fill_wide(p, HALF_FILL, 17), lambda: convolve(p, 0, 5), lambda: convolve(p, 5, 8))
 
     def regroup(p):
         def one(x):
@@ -522,7 +550,7 @@
             back.start(n_col - d)
         place(slot, jnp.concatenate(rounded, axis=0).astype(f32))
 
-    to_grid(first, lambda: first_fill(first), lambda: rest_of_conv(first), activate)
+    to_grid(first, lambda: first_fill(first), rest_of_conv(first), activate)
 
     piece = 80 // owners
 
@@ -621,7 +649,7 @@
 
     loop(32, one_channel)
     spread_mix([g.mixed_back[32 * part : 32 * part + 32].astype(bf16).astype(f32) * scale for part in range(2)])
-    to_grid(second, cover_rows_out, lambda: rest_of_conv(second), write_out)
+    to_grid(second, cover_rows_out, rest_of_conv(second), write_out)
 
     modes_ref[0] = first.modes[...]
     modes_ref[1] = second.modes[...]

time: 127 us -> 123 us (0.969); the launches traced: 127 us -> 121 us
  Pallas kernels: 126 us -> 121 us
    pallas_call x1, Pallas kernels: 121 us -> 115 us  [per_device(): pl.pallas_call(functools.partial(step_kernel, n_row, n_col, owners), out_...]
where the time goes in v9:
time: 123 us; the launch traced here: 121 us
  Pallas kernels  121 us (98%)
    pallas_call x1, Pallas kernels, per_device(): pl.pallas_call(functools.partial(step_kernel, n_row, n_col, owners), out_...  115 us
    pallas_call x1, Pallas kernels, per_device(): pl.pallas_call(outputs_kernel, out_shape=[jax.ShapeDtypeStruct((chans * r...  5.18 us

profile of v9, /device:TPU:1, one launch (start us, length us, event | category | flops | bytes accessed | tf_op | source)
XLA Modules:
  0.0 121.3 jit_solution(9578879963499719833)
XLA Ops:
  0.6 115.5 %layer_step.1 = (f32[2048,256]{1,0:T(8,128)}, f32[2,256,128]{2,1,0:T(8,128)}, f32[80,128]{1,0:T(8,128)}) custom-call(bf16[8,256,256]{2,1,0:T(8,128)(2,1)} %bitcast.9, bf16[64,256]{1,0:T(8,128)(2,1)} %refs_1_.1, bf16[288,32]{1,0:T(8,128)(2,1)} %bitcast.11, f32[1,32]{1,0:T(1,128)} %bitcast.12, f32[1,32]{1,0:T(1,128)} %bitcast.13, ...), custom_call_target="tpu_custom_call" | custom-call | tf_op jit(solution)/shard_map/layer_step/pallas_call | solution.py:714
  116.1 5.2 %layer_outputs.1 = (f32[2048,256]{1,0:T(8,128)}, f32[4,2,32,32,32]{4,3,2,1,0:T(8,128)}, f32[288,32]{1,0:T(8,128)}, f32[1,32]{1,0:T(1,128)}, f32[1,32]{1,0:T(1,128)}) custom-call(f32[2048,256]{1,0:T(8,128)} %get-tuple-element.13.cells_ref, f32[512,128]{1,0:T(8,128)} %bitcast.10, f32[80,128]{1,0:T(8,128)} %get-tuple-element.15.small_ref), custom_call_target="tpu_custom_call" | custom-call | tf_op jit(solution)/shard_map/layer_outputs/pallas_call | solution.py:738

commit v10 on v9

--- a/solution.py
+++ b/solution.py
@@ -12,7 +12,6 @@
 
 TWO_PI = 2.0 * math.pi
 HIGH = lax.Precision.HIGHEST
-HALF_FILL = 8
 VMEM_BYTES = 56 * 1024 * 1024
 
 
@@ -403,9 +402,9 @@
             use(block, dot(p.rcv10[block], g.ty[col_at], NN), (col_at - block) & (n_col - 1))
 
         p.rcv10[col_at] = lhs
+        send(2, col_at, beside)
         send(0, col_at, ahead)
         send(1, col_at, behind)
-        send(2, col_at, beside)
         cover_cells[0]()
         arrived(2, beside)
         send(3, beside, ahead)
@@ -419,7 +418,6 @@
         send(7, behind_beside, ahead, 0)
         arrived(4, ahead_beside)
         send(8, ahead_beside, behind, 1)
-        cover_cells[2]()
         use(col_at, dot(lhs, g.ty[col_at], NN), 0)
         ready = [beside, behind, ahead, behind_beside, ahead_beside]
         for block in ready:
@@ -434,10 +432,10 @@
     def first_fill(p):
         for copy in p.edge_copies:
             copy.wait_recv()
-        fill_wide(p, 0, HALF_FILL)
+        fill_wide(p, 0, 17)
 
     def rest_of_conv(p):
-        return (lambda: fill_wide(p, HALF_FILL, 17), lambda: convolve(p, 0, 5), lambda: convolve(p, 5, 8))
+        return (lambda: convolve(p, 0, 5), lambda: convolve(p, 5, 8))
 
     def regroup(p):
         def one(x):

time: 123 us -> 120 us (0.976)
  Pallas kernels: 121 us -> 119 us
    pallas_call x1, Pallas kernels: 115 us -> 114 us  [per_device(): pl.pallas_call(functools.partial(step_kernel, n_row, n_col, owners), out_...]
where the time goes in v10:
time: 120 us; the launch traced here: 119 us
  Pallas kernels  119 us (99%)
    pallas_call x1, Pallas kernels, per_device(): pl.pallas_call(functools.partial(step_kernel, n_row, n_col, owners), out_...  114 us
    pallas_call x1, Pallas kernels, per_device(): pl.pallas_call(outputs_kernel, out_shape=[jax.ShapeDtypeStruct((chans * r...  5.18 us

profile of v10, /device:TPU:1, one launch (start us, length us, event | category | flops | bytes accessed | tf_op | source)
XLA Modules:
  0.0 119.4 jit_solution(16059417598558422178)
XLA Ops:
  0.6 113.6 %layer_step.1 = (f32[2048,256]{1,0:T(8,128)}, f32[2,256,128]{2,1,0:T(8,128)}, f32[80,128]{1,0:T(8,128)}) custom-call(bf16[8,256,256]{2,1,0:T(8,128)(2,1)} %bitcast.9, bf16[64,256]{1,0:T(8,128)(2,1)} %refs_1_.1, bf16[288,32]{1,0:T(8,128)(2,1)} %bitcast.11, f32[1,32]{1,0:T(1,128)} %bitcast.12, f32[1,32]{1,0:T(1,128)} %bitcast.13, ...), custom_call_target="tpu_custom_call" | custom-call | tf_op jit(solution)/shard_map/layer_step/pallas_call | solution.py:712
  114.2 5.2 %layer_outputs.1 = (f32[2048,256]{1,0:T(8,128)}, f32[4,2,32,32,32]{4,3,2,1,0:T(8,128)}, f32[288,32]{1,0:T(8,128)}, f32[1,32]{1,0:T(1,128)}, f32[1,32]{1,0:T(1,128)}) custom-call(f32[2048,256]{1,0:T(8,128)} %get-tuple-element.13.cells_ref, f32[512,128]{1,0:T(8,128)} %bitcast.10, f32[80,128]{1,0:T(8,128)} %get-tuple-element.15.small_ref), custom_call_target="tpu_custom_call" | custom-call | tf_op jit(solution)/shard_map/layer_outputs/pallas_call | solution.py:736
